TPU v7x, 32 devices: a whole 2x2x4 slice. The times are simulated.
32 devices in a mesh: dp: 8 (over y, x, core), tensor: 4 (over z).
Axes of the slice: x: 2, y: 2, z: 4, core: 2. Of those that a mesh axis runs over, the one named last changes fastest.
Arguments:
- tokens: bfloat16 [16, 2048, 768], P('dp', 'tensor'), may hold values from -6 to 6
- segments: int32 [16, 2048], P('dp'), may hold values from 0 to 3, never falling along the last dimension, each value on 1 to 800 neighbouring positions
- pairing: int32 [12, 4], P('tensor'), may hold values from 0 to 3, each once within a row
- qkv_weight: bfloat16 [768, 12, 192], P('dp', 'tensor'), may hold values from -0.3125 to 0.3125
- qv_bias: bfloat16 [12, 128], P('tensor'), may hold values from -3 to 3
- out_weight: bfloat16 [12, 64, 768], P('tensor', None, 'dp'), may hold values from -0.875 to 0.875
- out_bias: bfloat16 [768], replicated, may hold values from -3 to 3
- first_gain: bfloat16 [768], replicated, may hold values from 0.5 to 1.5
- first_shift: bfloat16 [768], replicated, may hold values from -2 to 2
- up_weight: bfloat16 [768, 3072], P('dp', 'tensor'), may hold values from -0.21875 to 0.21875
- up_bias: bfloat16 [3072], P('tensor'), may hold values from -3 to 3
- down_weight: bfloat16 [3072, 768], P('tensor', 'dp'), may hold values from -0.109375 to 0.109375
- down_bias: bfloat16 [768], replicated, may hold values from -3 to 3
- second_gain: bfloat16 [768], replicated, may hold values from 0.5 to 1.5
- second_shift: bfloat16 [768], replicated, may hold values from -2 to 2
- cotangent: bfloat16 [16, 2048, 768], P('dp', 'tensor'), may hold values from -6 to 6
Outputs:
- layer_out: bfloat16 [16, 2048, 768], P('dp', 'tensor')
- input_grad: bfloat16 [16, 2048, 768], P('dp', 'tensor')
- qkv_weight_grad: float32 [768, 12, 192], P('dp', 'tensor')
- qv_bias_grad: float32 [12, 128], P('tensor')
- out_weight_grad: float32 [12, 64, 768], P('tensor', None, 'dp')
- out_bias_grad: float32 [768], replicated
- first_gain_grad: float32 [768], replicated
- first_shift_grad: float32 [768], replicated
- up_weight_grad: float32 [768, 3072], P('dp', 'tensor')
- up_bias_grad: float32 [3072], P('tensor')
- down_weight_grad: float32 [3072, 768], P('tensor', 'dp')
- down_bias_grad: float32 [768], replicated
- second_gain_grad: float32 [768], replicated
- second_shift_grad: float32 [768], replicated
Inputs may be any that keep to these rules, and one draw needn't show every extreme that they name: `segments`: along each sequence the numbers never fall; each number covers at most 800 positions of its sequence, and one covers exactly 800. `pairing`: each row holds every number from 0 to 3 once.
All inputs are finite; a program needn't handle non-finite values.
Results may differ from a plain program's by a relative error of at most 0.013.
Values may be sent and summed in bfloat16 or wider, within the bound.
No kernel may reach another device: no remote copies, remote signals or barrier semaphores. Data moves between devices by JAX's collectives and lax.ppermute only.
A program may use at most 192 MiB of HBM per device.

v0:
```python
import functools

import jax
import jax.numpy as jnp
from jax import lax
from jax.experimental import pallas as pl
from jax.experimental.pallas import tpu as pltpu
from jax.sharding import PartitionSpec as P

EPS = 1e-06
NEG = -1e30
BOTH = ("dp", "tensor")
F32 = jnp.float32
BF16 = jnp.bfloat16
ANY = pl.BlockSpec(memory_space=pl.ANY)
LIMIT = 58 << 20
COST = pl.CostEstimate(flops=10**9, bytes_accessed=1 << 16, transcendentals=0)


def mm(left, right):
    return lax.dot_general(left, right, (((1,), (0,)), ((), ())), preferred_element_type=F32)


def mm_rt(left, right):
    return lax.dot_general(left, right, (((1,), (1,)), ((), ())), preferred_element_type=F32)


def mm_lt(left, right):
    return lax.dot_general(left, right, (((0,), (0,)), ((), ())), preferred_element_type=F32)


def head_lanes(shape, head, dim, head_size):
    place = lax.broadcasted_iota(jnp.int32, shape, dim)
    return (place < head_size) if head == 0 else (place >= head_size)


def fetches(pieces, offsets, target, dim, sems, first):
    copies = []
    for k, (piece, offset) in enumerate(zip(pieces, offsets)):
        count = piece.shape[dim]
        where = pl.ds(offset if isinstance(offset, int) else pl.multiple_of(offset, count), count)
        index = (slice(None),) * dim + (where,)
        copies.append(pltpu.make_async_copy(piece, target.at[index], sems.at[first + k]))
    return copies


def piece_rows(place, step, rows, count):
    if count == 1:
        return [0]
    return [(place ^ (k * step)) * rows for k in range(count)]


def attend_kernel(pair_ref, place_ref, *refs, rows, hs, blocks, n_w):
    x_refs, refs = refs[:2], refs[2:]
    w_refs, refs = refs[:n_w], refs[n_w:]
    bias_ref, segq_ref, segk_ref, q_out, k_out, v_out, o_mine, o_other, lse_ref, w_all, x_all, sems = refs
    group, block = pl.program_id(0), pl.program_id(1)
    lanes2 = 2 * hs

    @pl.when((group == 0) & (block == 0))
    def _():
        chip = place_ref[0] // 2
        w_parts = [piece.at[: w_all.shape[0]] for piece in w_refs]
        copies = fetches(
            w_parts, piece_rows(chip, 1, w_refs[0].shape[1], n_w), w_all, 1, sems, 0
        ) + fetches(x_refs, [0, x_refs[0].shape[0]], x_all, 0, sems, n_w)
        for copy in copies:
            copy.start()
        for copy in copies:
            copy.wait()

    @pl.when(block == 0)
    def _():
        weight = w_all[group]
        for k in range(blocks):
            part = pl.ds(k * rows, rows)
            out = (mm(x_all[part, :], weight) + bias_ref[0]).astype(BF16)
            q_out[part, :] = out[:, :lanes2] * (hs**-0.5)
            k_out[part, :] = out[:, lanes2 : 2 * lanes2]
            v_out[part, :] = out[:, 2 * lanes2 :]

    own = pl.ds(pl.multiple_of(block * rows, rows), rows)
    q2 = q_out[own, :]
    own_raw = (q2.astype(F32) * k_out[own, :].astype(F32)).T
    own_values = v_out[own, :].astype(F32).T
    segq = segq_ref[...]
    total = jnp.zeros((2 * hs, rows), F32)
    for head in range(2):
        target = pair_ref[2 * group + head, block]
        there = pl.ds(pl.multiple_of(target * rows, rows), rows)
        keys, values = k_out[there, :], v_out[there, :]
        lanes = head_lanes(q2.shape, head, 1, hs)
        scores = mm_rt(keys, jnp.where(lanes, q2, jnp.zeros_like(q2)))
        scores = jnp.where(segk_ref[there, :] == segq, scores, NEG)
        raw = jnp.sum(own_raw[head * hs : (head + 1) * hs], axis=0, keepdims=True)
        raw = jnp.where(target != block, raw, NEG)
        peak = jnp.maximum(jnp.max(scores, axis=0, keepdims=True), raw)
        expo = jnp.exp(scores - peak)
        own_expo = jnp.exp(raw - peak)
        denom = jnp.sum(expo, axis=0, keepdims=True) + own_expo
        masked_values = jnp.where(lanes, values, jnp.zeros_like(values))
        part = mm_lt(masked_values, expo.astype(BF16))
        low = own_expo.astype(BF16).astype(F32)
        mine = head_lanes(part.shape, head, 0, hs)
        part = part + jnp.where(mine, own_values * low, 0.0)
        total = total + part * (1.0 / denom)
        lse_ref[0, head : head + 1, :] = peak + jnp.log(denom)
    mixed = total.T.astype(BF16)

    @pl.when(block < blocks // 2)
    def _():
        o_mine[pl.ds(pl.multiple_of(block * rows, rows), rows), :] = mixed

    @pl.when(block >= blocks // 2)
    def _():
        o_other[pl.ds(pl.multiple_of((block - blocks // 2) * rows, rows), rows), :] = mixed


def attend(pairs, place, x_parts, w_pieces, bias, segq, segk, hs):
    heads, blocks = pairs.shape
    width = x_parts[0].shape[1]
    seq, groups, lanes = 2 * x_parts[0].shape[0], heads // 2, 2 * hs
    rows = seq // blocks
    kept = jax.ShapeDtypeStruct((seq, groups * lanes), BF16)
    flops = 2 * seq * width * 3 * groups * lanes + 4 * heads * seq * rows * 2 * lanes
    return pl.pallas_call(
        functools.partial(attend_kernel, rows=rows, hs=hs, blocks=blocks, n_w=len(w_pieces)),
        grid_spec=pltpu.PrefetchScalarGridSpec(
            num_scalar_prefetch=2,
            grid=(groups, blocks),
            in_specs=[ANY] * (2 + len(w_pieces))
            + [
                pl.BlockSpec((1, 1, 3 * lanes), lambda g, i, p, q: (g, 0, 0)),
                pl.BlockSpec((1, rows), lambda g, i, p, q: (0, i)),
                pl.BlockSpec((seq, 1), lambda g, i, p, q: (0, 0)),
            ],
            out_specs=[pl.BlockSpec((seq, lanes), lambda g, i, p, q: (0, g))] * 3
            + [
                pl.BlockSpec((seq // 2, lanes), lambda g, i, p, q: (0, g)),
                pl.BlockSpec((seq // 2, lanes), lambda g, i, p, q: (0, g)),
                pl.BlockSpec((1, 8, rows), lambda g, i, p, q: (g, 0, i)),
                pl.BlockSpec((groups, width, 3 * lanes), lambda g, i, p, q: (0, 0, 0)),
            ],
            scratch_shapes=[
                pltpu.VMEM((seq, width), BF16),
                pltpu.SemaphoreType.DMA((2 + len(w_pieces),)),
            ],
        ),
        out_shape=[kept] * 3
        + [jax.ShapeDtypeStruct((seq // 2, groups * lanes), BF16)] * 2
        + [
            jax.ShapeDtypeStruct((groups, 8, seq), F32),
            jax.ShapeDtypeStruct((groups, width, 3 * lanes), BF16),
        ],
        compiler_params=pltpu.CompilerParams(vmem_limit_bytes=58 << 20),
        cost_estimate=COST,
        name="attend",
    )(pairs, place, *x_parts, *w_pieces, bias, segq, segk)


def attend_back_kernel(
    pair_ref, group_ref, q_ref, k_ref, v_ref, do_a, do_b, segq_ref, segk_ref, lse_ref,
    packed_ref, sums_ref, dq_all, dk_acc, dv_acc, *, rows, hs, blocks,
):
    block = pl.program_id(0)

    @pl.when(block == 0)
    def _():
        dk_acc[...] = jnp.zeros_like(dk_acc)
        dv_acc[...] = jnp.zeros_like(dv_acc)
        sums_ref[...] = jnp.zeros_like(sums_ref)

    own = pl.ds(pl.multiple_of(block * rows, rows), rows)
    q2, do2 = q_ref[...], jnp.where(block < blocks // 2, do_a[...], do_b[...])
    qt, dot = q2.astype(F32).T, do2.astype(F32).T
    own_keys, own_values = k_ref[own, :].astype(F32).T, v_ref[own, :].astype(F32).T
    own_raw, own_dp = qt * own_keys, dot * own_values
    segq = segq_ref[...]
    dq = jnp.zeros((2 * hs, rows), F32)
    own_ds, own_low = [], []
    for head in range(2):
        target = pair_ref[2 * group_ref[0] + head, block]
        there = pl.ds(pl.multiple_of(target * rows, rows), rows)
        keys, values = k_ref[there, :], v_ref[there, :]
        lanes = head_lanes(q2.shape, head, 1, hs)
        zero = jnp.zeros_like(q2)
        qm, dom = jnp.where(lanes, q2, zero), jnp.where(lanes, do2, zero)
        lse = lse_ref[0, head : head + 1, :]
        scores = mm_rt(keys, qm)
        probs = jnp.exp(jnp.where(segk_ref[there, :] == segq, scores - lse, NEG))
        raw = jnp.sum(own_raw[head * hs : (head + 1) * hs], axis=0, keepdims=True)
        self_prob = jnp.exp(jnp.where(target != block, raw - lse, NEG))
        self_dp = jnp.sum(own_dp[head * hs : (head + 1) * hs], axis=0, keepdims=True)
        dv_acc[there, :] += mm(probs.astype(BF16), dom)
        dprobs = mm_rt(values, dom)
        delta = jnp.sum(probs * dprobs, axis=0, keepdims=True) + self_prob * self_dp
        dscores = (probs * (dprobs - delta)).astype(BF16)
        dk_acc[there, :] += mm(dscores, qm)
        dq = dq + mm_lt(jnp.where(lanes, keys, jnp.zeros_like(keys)), dscores)
        own_ds.append((self_prob * (self_dp - delta)).astype(BF16).astype(F32))
        own_low.append(self_prob.astype(BF16).astype(F32))
    first = head_lanes(dq.shape, 0, 0, hs)
    ds_rows = jnp.where(first, own_ds[0], own_ds[1])
    low_rows = jnp.where(first, own_low[0], own_low[1])
    dq = ((dq + ds_rows * own_keys) * (hs**-0.5)).T
    dq_all[own, :] = dq.astype(BF16)
    sums_ref[0:1, :] += jnp.sum(dq, axis=0, keepdims=True)
    dk_acc[own, :] += (ds_rows * qt).T
    dv_acc[own, :] += (low_rows * dot).T

    @pl.when(block == blocks - 1)
    def _():
        dv = dv_acc[...]
        sums_ref[1:2, :] = jnp.sum(dv, axis=0, keepdims=True)
        packed_ref[...] = jnp.concatenate(
            [dq_all[...], dk_acc[...].astype(BF16), dv.astype(BF16)], axis=1
        )


def attend_back(pairs, group, q, k, v, grad_a, grad_b, segq, segk, lse, hs):
    heads, blocks = pairs.shape
    seq, lanes = q.shape[0], 2 * hs
    rows, half = seq // blocks, blocks // 2
    return pl.pallas_call(
        functools.partial(attend_back_kernel, rows=rows, hs=hs, blocks=blocks),
        grid_spec=pltpu.PrefetchScalarGridSpec(
            num_scalar_prefetch=2,
            grid=(blocks,),
            in_specs=[
                pl.BlockSpec((rows, lanes), lambda i, p, g: (i, g[0])),
                pl.BlockSpec((seq, lanes), lambda i, p, g: (0, g[0])),
                pl.BlockSpec((seq, lanes), lambda i, p, g: (0, g[0])),
                pl.BlockSpec((rows, lanes), lambda i, p, g: (jnp.minimum(i, half - 1), g[0])),
                pl.BlockSpec((rows, lanes), lambda i, p, g: (jnp.maximum(i - half, 0), g[0])),
                pl.BlockSpec((1, rows), lambda i, p, g: (0, i)),
                pl.BlockSpec((seq, 1), lambda i, p, g: (0, 0)),
                pl.BlockSpec((1, 8, rows), lambda i, p, g: (g[0], 0, i)),
            ],
            out_specs=[
                pl.BlockSpec((seq, 3 * lanes), lambda i, p, g: (0, 0)),
                pl.BlockSpec((8, lanes), lambda i, p, g: (0, 0)),
            ],
            scratch_shapes=[
                pltpu.VMEM((seq, lanes), BF16),
                pltpu.VMEM((seq, lanes), F32),
                pltpu.VMEM((seq, lanes), F32),
            ],
        ),
        out_shape=[
            jax.ShapeDtypeStruct((seq, 3 * lanes), BF16),
            jax.ShapeDtypeStruct((8, lanes), F32),
        ],
        compiler_params=pltpu.CompilerParams(vmem_limit_bytes=12 << 20),
        cost_estimate=COST,
        name="attend_back",
    )(pairs, jnp.full((1,), group, jnp.int32), q, k, v, grad_a, grad_b, segq, segk, lse)


def qkv_grad_kernel(place_ref, *refs):
    packed_refs, xa_ref, xb_ref, keep_ref, send_a, send_b, packed, acc, sems = refs[:3], *refs[3:]
    half = xa_ref.shape[0]
    chip = place_ref[0] // 2
    rows = keep_ref.shape[2]
    step = pl.program_id(0)
    copies = [
        pltpu.make_async_copy(packed_refs[g], packed.at[j], sems.at[j]) for j, g in enumerate((0, 2, 1))
    ]

    @pl.when(step == 0)
    def _():
        for copy in copies:
            copy.start()

    for j, copy in enumerate(copies):

        @pl.when(step == j)
        def _(copy=copy):
            copy.wait()

    acc[...] = mm_lt(xa_ref[...], packed[step, :half, :]) + mm_lt(xb_ref[...], packed[step, half:, :])
    for k, away in enumerate(away_of(step == 2)):
        ours = acc[pl.ds(pl.multiple_of((chip ^ away) * rows, rows), rows), :]
        if k < 2:
            keep_ref[0, k] = ours
        else:
            ours = ours.astype(BF16)

            @pl.when(step < 2)
            def _(ours=ours, k=k):
                send_a[0, k - 2] = ours

            @pl.when(step == 2)
            def _(ours=ours, k=k):
                send_b[0, k - 2] = ours


def qkv_grads(place, x_parts, packed, rows):
    half, width = x_parts[0].shape
    cols = packed[0].shape[1]
    whole = lambda a, b: pl.BlockSpec((a, b), lambda i, p: (0, 0))
    return pl.pallas_call(
        qkv_grad_kernel,
        grid_spec=pltpu.PrefetchScalarGridSpec(
            num_scalar_prefetch=1,
            grid=(3,),
            in_specs=[ANY] * 3 + [whole(half, width)] * 2,
            out_specs=[
                pl.BlockSpec((1, 2, rows, cols), lambda i, p: (i, 0, 0, 0)),
                pl.BlockSpec((1, 2, rows, cols), lambda i, p: (jnp.minimum(i, 1), 0, 0, 0)),
                pl.BlockSpec((1, 2, rows, cols), lambda i, p: (0, 0, 0, 0)),
            ],
            scratch_shapes=[
                pltpu.VMEM((3, 2 * half, cols), BF16),
                pltpu.VMEM((width, cols), F32),
                pltpu.SemaphoreType.DMA((3,)),
            ],
        ),
        out_shape=[
            jax.ShapeDtypeStruct((3, 2, rows, cols), F32),
            jax.ShapeDtypeStruct((2, 2, rows, cols), BF16),
            jax.ShapeDtypeStruct((1, 2, rows, cols), BF16),
        ],
        compiler_params=pltpu.CompilerParams(vmem_limit_bytes=18 << 20),
        cost_estimate=COST,
        name="qkv_grads",
    )(place, *packed, *x_parts)


def in_grad_kernel(*refs, n, half):
    packed, w_ref, extra, mine_ref, other_ref = refs[:n], refs[n], *refs[n + 1 :]
    step = pl.program_id(0)
    total = mm_rt(packed[0][...], w_ref[0])
    for g in range(1, n):
        total = total + mm_rt(packed[g][...], w_ref[g])

    @pl.when(step < half)
    def _():
        other_ref[...] = total.astype(BF16)

    @pl.when(step >= half)
    def _():
        mine_ref[...] = total + extra[...]


def in_grad(packed, weight, extra):
    seq, cols = packed[0].shape
    n, width = weight.shape[:2]
    half = 2
    tile = seq // (2 * half)
    late = lambda i: (jnp.maximum(i - half, 0), 0)
    return pl.pallas_call(
        functools.partial(in_grad_kernel, n=n, half=half),
        grid=(2 * half,),
        in_specs=[pl.BlockSpec((tile, cols), lambda i: ((i + half) % (2 * half), 0))] * n
        + [pl.BlockSpec((n, width, cols), lambda i: (0, 0, 0)), pl.BlockSpec((tile, width), late)],
        out_specs=[
            pl.BlockSpec((tile, width), late),
            pl.BlockSpec((tile, width), lambda i: (jnp.minimum(i, half - 1), 0)),
        ],
        out_shape=[
            jax.ShapeDtypeStruct((seq // 2, width), F32),
            jax.ShapeDtypeStruct((seq // 2, width), BF16),
        ],
        compiler_params=pltpu.CompilerParams(vmem_limit_bytes=12 << 20),
        cost_estimate=COST,
        name="in_grad",
    )(*packed, weight, extra)


def norm(values):
    centred = values - jnp.mean(values, axis=-1, keepdims=True)
    scale = lax.rsqrt(jnp.mean(centred * centred, axis=-1, keepdims=True) + EPS)
    return centred * scale, scale


def norm_back(grad, unit, scale, gain):
    q = grad * gain
    mean_q = jnp.mean(q, axis=-1, keepdims=True)
    mean_qn = jnp.mean(q * unit, axis=-1, keepdims=True)
    return scale * (q - mean_q - unit * mean_qn)


def gelu_parts(u):
    dense = jnp.exp(-0.5 * u * u) * 0.3989422804014327
    t = 1.0 / (1.0 + 0.2316419 * jnp.abs(u))
    poly = t * (
        0.319381530
        + t * (-0.356563782 + t * (1.781477937 + t * (-1.821255978 + t * 1.330274429)))
    )
    tail = dense * poly
    phi = jnp.where(u >= 0, 1.0 - tail, tail)
    return u * phi, phi + u * dense


def dense_copies(place, pieces, wo, ww, sems):
    copies = []

    def add(source, target):
        copies.append(pltpu.make_async_copy(source, target, sems.at[len(copies)]))

    if len(pieces) == 2:
        add(pieces[0], wo)
        add(pieces[1], ww)
        return copies
    core, chip = place % 2, place // 2
    chips, rows, cols = pieces[0].shape
    for side in range(2):
        lanes = pl.ds(pl.multiple_of((core ^ side) * cols, cols), cols)
        for k in range(chips):
            add(pieces[side].at[k], wo.at[pl.ds(pl.multiple_of((chip ^ k) * rows, rows), rows), lanes])
    half, rows = pieces[2].shape[1:3]
    for k, piece in enumerate(pieces[2:]):
        away = ((0, 1), (0, 2), (2, 3), (1, 3))[k % 4]
        for j in range(2):
            base = (place ^ (2 * away[j] + k // 4)) * rows
            add(piece.at[j], ww.at[pl.ds((k % 2) * half, half), pl.ds(pl.multiple_of(base, rows), rows), :])
    return copies


def dense_kernel(place_ref, *refs, n_w, chunks):
    w_refs, refs = refs[:n_w], refs[n_w:]
    (
        x_ref, mine_ref, other_ref, cot_a, cot_b, vec_ref, upb_ref,
        layer_a, layer_b, gm_mine, gm_other, act_ref, mlow_ref, gb_ref, gul_ref, ga_ref, gone_ref, sums_ref,
        wo, ww, slope, layer, sems,
    ) = refs
    step = pl.program_id(0)
    core = place_ref[0] % 2
    cols = mine_ref.shape[1]
    width = x_ref.shape[1]
    units = ww.shape[2] // 2
    copies = dense_copies(place_ref[0], w_refs, wo, ww, sems)
    n_wo = 1 if len(w_refs) == 2 else 2 * w_refs[0].shape[0]

    @pl.when(step == 0)
    def _():
        for copy in copies:
            copy.start()
        for copy in copies[:n_wo]:
            copy.wait()
        sums_ref[...] = jnp.zeros_like(sums_ref)

    mine_cols = pl.ds(pl.multiple_of(core * cols, cols), cols)
    other_cols = pl.ds(pl.multiple_of((1 - core) * cols, cols), cols)
    early = step < pl.num_programs(0) // 2

    def add_sum(row, values):
        sums_ref[pl.ds(row, 1), :] += jnp.sum(values, axis=0, keepdims=True)

    def advance(at):
        attn = mm_rt(mine_ref[at, :], wo[:, mine_cols]) + mm_rt(other_ref[at, :], wo[:, other_cols])
        yield
        unit_one, scale_one = norm(x_ref[at, :].astype(F32) + attn + vec_ref[0:1, :])
        middle = unit_one * vec_ref[1:2, :] + vec_ref[2:3, :]
        low = middle.astype(BF16)
        mlow_ref[at, :] = low
        total = middle + vec_ref[3:4, :]

        @pl.when(step == 0)
        def _():
            for copy in copies[n_wo:]:
                copy.wait()

        yield
        for k in range(chunks):
            place = slice(k * units, (k + 1) * units)
            upper = mm(low, ww[k, :, :units]) + upb_ref[:, place]
            active, rise = gelu_parts(upper)
            active = active.astype(BF16)
            act_ref[at, place] = active
            slope[at, place] = rise.astype(BF16)
            total = total + mm_rt(active, ww[k, :, units:])
            yield
        unit_two, scale_two = norm(total)
        gain_two = vec_ref[4:5, :]
        layer[at, :] = (unit_two * gain_two + vec_ref[5:6, :]).astype(BF16)
        cot = jnp.where(early, cot_a[at, :], cot_b[at, :]).astype(F32)
        grad_two = norm_back(cot, unit_two, scale_two, gain_two)
        add_sum(4, cot * unit_two)
        add_sum(5, cot)
        add_sum(3, grad_two)
        low = grad_two.astype(BF16)
        gb_ref[at, :] = low
        total = grad_two
        yield
        for k in range(chunks):
            place = slice(k * units, (k + 1) * units)
            grad_upper = mm(low, ww[k, :, units:]) * slope[at, place].astype(F32)
            add_sum(8 + (k ^ place_ref[1]), grad_upper)
            grad_low = grad_upper.astype(BF16)
            gul_ref[at, place] = grad_low
            total = total + mm_rt(grad_low, ww[k, :, :units])
            yield
        add_sum(1, total * unit_one)
        add_sum(2, total)
        grad_one = norm_back(total, unit_one, scale_one, vec_ref[1:2, :])
        add_sum(0, grad_one)
        gone_ref[at, :] = grad_one
        grad_attn = grad_one.astype(BF16)
        ga_ref[at, :] = grad_attn
        yield
        gm_mine[at, :] = mm(grad_attn, wo[:, mine_cols]).astype(BF16)
        gm_other[at, :] = mm(grad_attn, wo[:, other_cols]).astype(BF16)
        yield

    part = x_ref.shape[0] // 1
    for _ in zip(*[advance(slice(part * k, part * (k + 1))) for k in range(1)]):
        pass

    @pl.when(early)
    def _():
        layer_a[...] = layer[...]

    @pl.when(jnp.logical_not(early))
    def _():
        layer_b[...] = layer[...]


def dense(place, w_pieces, x, mine, other, cot_a, cot_b, vec, upb, tile):
    count, width = x.shape
    cols = other.shape[1]
    units = w_pieces[-1].shape[-1] // 2
    chunks = upb.shape[1] // units
    steps = count // tile
    half = steps // 2
    n_copies = 2 if len(w_pieces) == 2 else 2 * w_pieces[0].shape[0] + 2 * (len(w_pieces) - 2)
    rows = lambda n: pl.BlockSpec((tile, n), lambda i, p: (i, 0))
    fixed = lambda a, b: pl.BlockSpec((a, b), lambda i, p: (0, 0))
    full = chunks * units
    shapes = [
        ((count // 2, width), BF16), ((count // 2, width), BF16),
        ((count, cols), BF16), ((count, cols), BF16), ((count, full), BF16),
        ((count, width), BF16), ((count, width), BF16), ((count, full), BF16), ((count, width), BF16),
        ((count, width), F32), ((16, width), F32),
    ]
    flops = 8 * count * width * full + 4 * count * width * 2 * cols
    return pl.pallas_call(
        functools.partial(dense_kernel, n_w=len(w_pieces), chunks=chunks),
        grid_spec=pltpu.PrefetchScalarGridSpec(
            num_scalar_prefetch=1,
            grid=(count // tile,),
            in_specs=[ANY] * len(w_pieces)
            + [rows(width), rows(cols), rows(cols)]
            + [
                pl.BlockSpec((tile, width), lambda i, p: (jnp.minimum(i, half - 1), 0)),
                pl.BlockSpec((tile, width), lambda i, p: (jnp.maximum(i - half, 0), 0)),
                fixed(8, width),
                fixed(1, full),
            ],
            out_specs=[
                pl.BlockSpec((tile, width), lambda i, p: (jnp.minimum(i, half - 1), 0)),
                pl.BlockSpec((tile, width), lambda i, p: (jnp.maximum(i - half, 0), 0)),
                rows(cols), rows(cols), rows(full), rows(width), rows(width), rows(full),
                rows(width), rows(width), fixed(16, width),
            ],
            scratch_shapes=[
                pltpu.VMEM((width, 2 * cols), BF16),
                pltpu.VMEM((chunks, width, 2 * units), BF16),
                pltpu.VMEM((tile, full), BF16),
                pltpu.VMEM((tile, width), BF16),
                pltpu.SemaphoreType.DMA((n_copies,)),
            ],
        ),
        out_shape=[jax.ShapeDtypeStruct(*s) for s in shapes],
        compiler_params=pltpu.CompilerParams(vmem_limit_bytes=27 << 20),
        cost_estimate=COST,
        name="dense",
    )(place, *w_pieces, x, mine, other, cot_a, cot_b, vec, upb)


def away_of(second):
    return [0, jnp.where(second, 1, 2), jnp.where(second, 2, 1), 3]


def grad_kernel(place_ref, *refs, n, steps, drows, first):
    left_ref, right_ref, refs = refs[0], refs[1], refs[2:]
    extra, (keep_ref, send_ref, theirs_ref, left_t, acc) = refs[: n - 2], refs[n - 2 :]
    core, chip = place_ref[0] % 2, place_ref[0] // 2
    step = pl.program_id(0)

    @pl.when(step == 0)
    def _():
        left_t[...] = left_ref[...].T

    @pl.when(step >= steps)
    def _():
        acc[...] = mm(left_t[...], right_ref[...])

    if extra:

        @pl.when(step < steps)
        def _():
            cols = extra[1].shape[1]
            mine_cols = pl.ds(pl.multiple_of(core * cols, cols), cols)
            other_cols = pl.ds(pl.multiple_of((1 - core) * cols, cols), cols)
            acc[:, mine_cols] = mm_lt(extra[0][...], extra[1][...])
            acc[:, other_cols] = mm_lt(extra[0][...], extra[2][...])

    for k, away in enumerate(away_of(step >= first)):
        base = 2 * (chip ^ away)
        ours = acc[pl.ds(pl.multiple_of((base + core) * drows, drows), drows), :]
        if k < 2:
            keep_ref[0, k] = ours
        else:
            send_ref[0, k - 2] = ours.astype(BF16)
        theirs_ref[0, k] = acc[pl.ds(pl.multiple_of((base + 1 - core) * drows, drows), drows), :].astype(BF16)


def weight_grad(place, left, right, extra, drows, first):
    count, width = left.shape
    tile = width
    steps = 1 if extra else 0
    chunks = right.shape[1] // tile + steps
    whole = lambda a, b: pl.BlockSpec((a, b), lambda i, p: (0, 0))
    shapes = [((chunks, 2, drows, tile), F32), ((chunks, 2, drows, tile), BF16), ((chunks, 4, drows, tile), BF16)]
    return pl.pallas_call(
        functools.partial(grad_kernel, n=2 + len(extra), steps=steps, drows=drows, first=first),
        grid_spec=pltpu.PrefetchScalarGridSpec(
            num_scalar_prefetch=1,
            grid=(chunks,),
            in_specs=[
                whole(count, width),
                pl.BlockSpec((count, tile), lambda i, p: (0, jnp.maximum(i - steps, 0))),
            ]
            + [whole(count, e.shape[1]) for e in extra],
            out_specs=[pl.BlockSpec((1,) + shape[1:], lambda i, p: (i, 0, 0, 0)) for shape, _ in shapes],
            scratch_shapes=[pltpu.VMEM((width, count), BF16), pltpu.VMEM((width, tile), F32)],
        ),
        out_shape=[jax.ShapeDtypeStruct(*shape) for shape in shapes],
        compiler_params=pltpu.CompilerParams(vmem_limit_bytes=15 << 20),
        cost_estimate=COST,
        name="weight_grad",
    )(place, left, right, *extra)


def xor_order(parts, index):
    parts = list(parts)
    bit = 1
    while bit < len(parts):
        odd = (index // bit) % 2 == 1
        parts = [jnp.where(odd, parts[k ^ bit], parts[k]) for k in range(len(parts))]
        bit *= 2
    return parts


def per_device(
    tokens,
    segments,
    pairing,
    qkv_weight,
    qv_bias,
    out_weight,
    out_bias,
    first_gain,
    first_shift,
    up_weight,
    up_bias,
    down_weight,
    down_bias,
    second_gain,
    second_shift,
    cotangent,
):
    width = tokens.shape[2]
    rows = tokens.shape[1]
    lheads, blocks = pairing.shape
    hs = qv_bias.shape[1] // 2
    lanes = 2 * hs
    units = up_weight.shape[1]
    ndp, nt = lax.axis_size("dp"), lax.axis_size("tensor")
    drows = width // ndp
    chips = ndp // 2
    dp, tensor = lax.axis_index("dp"), lax.axis_index("tensor")
    core, chip, half, low = dp % 2, dp // 2, tensor // 2, tensor % 2
    slot_mask = 2 * core + low
    heads = 2 * lheads
    cols = heads * hs
    aligned = drows % 8 == 0
    place = jnp.stack([dp, tensor]).astype(jnp.int32)
    order = [0, 1, 3, 4, 2, 5]

    core_pairs = [(i, i ^ 1) for i in range(ndp)]

    def core_swap(x):
        return lax.ppermute(x, "dp", core_pairs)

    def z_step(x, k):
        return lax.ppermute(x, "tensor", [(i, i ^ k) for i in range(nt)])

    def chip_step(x, k):
        return lax.ppermute(x, "dp", [(i, i ^ (2 * k)) for i in range(ndp)])

    def column(k, flip, back):
        steps = []
        for p in range(chips):
            for c in range(2):
                for a in range(2):
                    for b in range(2):
                        home = (2 * p + c) * nt + 2 * a + b
                        away = (2 * p + (a ^ flip)) * nt + 2 * c + (b ^ k)
                        steps.append((away, home) if back else (home, away))
        return steps

    def of_sequence(x, k):
        return lax.dynamic_index_in_dim(x, low ^ k, 0, keepdims=False)

    def to_sequence(part, k):
        return lax.ppermute(part, BOTH, column(k, 0, False))

    def at_home(first, second):
        return jnp.stack([jnp.where(low == 0, first, second), jnp.where(low == 0, second, first)])

    def z_all(x):
        return [x] + [z_step(x, k) for k in range(1, nt)]

    def chip_all(x):
        return [x] + [chip_step(x, k) for k in range(1, chips)]

    gate = lambda *trees: lax.optimization_barrier(trees)

    qkv_local = qkv_weight.reshape(drows, lheads, 3, hs).transpose(0, 2, 1, 3)
    qkv_local = jnp.concatenate(
        [
            qkv_local[:, :, :2].reshape(drows, 3 * lanes),
            qkv_local[:, :, 2].reshape(drows, 3 * hs),
            out_weight.reshape(lheads * hs, drows).T,
        ],
        axis=1,
    )
    small = jnp.concatenate([pairing.astype(BF16).reshape(-1), qv_bias.reshape(-1), up_bias])
    n_pair, n_qv = lheads * blocks, lheads * lanes
    extra_rows = 8
    small = jnp.pad(small, (0, extra_rows * qkv_local.shape[1] - small.shape[0]))
    first_z = z_all(jnp.concatenate([qkv_local, small.reshape(extra_rows, -1)]))
    segs = jnp.where(half == core, segments, core_swap(segments))
    ff_local = jnp.concatenate([up_weight, down_weight.T], axis=1)
    ff_local, first_z = gate(ff_local, first_z)
    ff_one = z_step(ff_local, 1)

    abs_z = xor_order([part[:drows] for part in first_z], tensor)
    qkv_cols = 3 * lheads * hs

    def regroup(first, second):
        left, right = first[:, 3 * lanes : qkv_cols], second[:, 3 * lanes : qkv_cols]
        both = [part[:, hs * k : hs * (k + 1)] for k in range(3) for part in (left, right)]
        return jnp.stack([first[:, : 3 * lanes], second[:, : 3 * lanes], jnp.concatenate(both, axis=1)])

    def with_out(first, second):
        left, right = first[:, qkv_cols:], second[:, qkv_cols:]
        out = jnp.concatenate([left[:, :lanes], right[:, :lanes], left[:, lanes:], right[:, lanes:]], axis=1)
        return jnp.concatenate([regroup(first, second), out[None]])

    zero_heads, one_heads = with_out(abs_z[0], abs_z[1]), with_out(abs_z[2], abs_z[3])
    keep = jnp.where(core == 0, zero_heads, one_heads)
    got = core_swap(jnp.where(core == 0, one_heads, zero_heads))
    chip_rows = jnp.where(
        core == 0, jnp.concatenate([keep, got], axis=1), jnp.concatenate([got, keep], axis=1)
    )
    ff_pair = jnp.stack([ff_local, ff_one])
    chip_rows, ff_pair = gate(chip_rows, ff_pair)
    qkv_pieces = chip_all(chip_rows)
    ff_middle = lax.ppermute(ff_pair, "tensor", [(1, 2), (2, 1)])

    tokens, ff_middle = gate(tokens, ff_middle)
    ff_end = lax.ppermute(ff_middle, "tensor", [(1, 0), (2, 3)])
    moved = [to_sequence(of_sequence(tokens, k), k) for k in range(2)]
    inner = (tensor == 1) | (tensor == 2)
    ff_other = jnp.where(inner, ff_middle[::-1], ff_end)
    qkv_pieces, ff_pair, ff_other, moved[0] = gate(qkv_pieces, ff_pair, ff_other, moved[0])
    out_mine = jnp.stack([piece[3] for piece in qkv_pieces])
    if aligned:
        firsts = [chip_step(ff_pair, 1), chip_step(ff_other, 2)]
        twos = [jnp.stack([ff_pair, firsts[0]]), jnp.stack([ff_other, firsts[1]])]
        cots = [of_sequence(cotangent, k) for k in range(2)]
        twos, moved, cots = gate(twos, moved, cots)
        fours = [chip_step(twos[0], 2), chip_step(twos[1], 1)]
        x_mine = jnp.concatenate(moved)
        x_other = core_swap(x_mine)
        twos_swapped = [core_swap(two) for two in twos]
        cots, x_mine, x_other, twos_swapped = gate(cots, x_mine, x_other, twos_swapped)
        cot_a, cot_b = [to_sequence(part, k) for k, part in enumerate(cots)]
    else:
        x_mine = jnp.concatenate(moved)
        x_other = core_swap(x_mine)
        cot_a, cot_b = [to_sequence(of_sequence(cotangent, k), k) for k in range(2)]
        out_other = core_swap(out_mine)
        ff_own = chip_all(jnp.concatenate([ff_pair, ff_other]))
        ff_all = [part for piece in ff_own for part in (piece, core_swap(piece))]
        qkv_pieces = [jnp.concatenate(xor_order(qkv_pieces, chip), axis=1)]
        out_both = [jnp.concatenate(xor_order(list(o), chip)) for o in (out_mine, out_other)]
        dense_pieces = [
            jnp.concatenate(
                [jnp.where(core == 0, out_both[0], out_both[1]), jnp.where(core == 0, out_both[1], out_both[0])],
                axis=1,
            ),
            jnp.concatenate(xor_order(ff_all, dp), axis=1),
        ]

    small_rel = [part[drows:].reshape(-1) for part in first_z]
    small = jnp.stack(xor_order(small_rel, tensor))
    all_pairs = small[:, :n_pair].astype(jnp.int32).reshape(2, heads, blocks)
    my_pairs = jnp.where(core == 0, all_pairs[0], all_pairs[1])
    pair_slots = jnp.stack(xor_order([my_pairs[:, k] for k in range(blocks)], slot_mask), axis=1) ^ slot_mask
    pair_slots = jnp.stack([pair_slots[h] for h in order])
    all_qvb = small[:, n_pair : n_pair + n_qv].astype(F32).reshape(2, heads, lanes)
    my_qvb = jnp.where(core == 0, all_qvb[0], all_qvb[1])
    my_qvb = jnp.stack([my_qvb[h] for h in order])
    up_bias_rel = jnp.concatenate([s[n_pair + n_qv :][:units] for s in small_rel]).astype(F32)
    groups = heads // 2
    bias = jnp.concatenate(
        [
            my_qvb[:, :hs].reshape(groups, lanes),
            jnp.zeros((groups, lanes), F32),
            my_qvb[:, hs:].reshape(groups, lanes),
        ],
        axis=1,
    ).reshape(groups, 1, 3 * lanes)

    seg_rows = jnp.where(low == 0, segs[0], segs[1]).reshape(blocks, rows)
    seg_row = jnp.concatenate(xor_order([seg_rows[k] for k in range(blocks)], slot_mask))
    seg_col = seg_row.reshape(blocks * rows, 1)
    seg_row = seg_row.reshape(1, blocks * rows)

    x_parts = [x_mine, x_other]
    q, k, v, mixed, mixed_other, lse, w_all = attend(pair_slots, place, x_parts, qkv_pieces, bias, seg_row, seg_col, hs)
    if aligned:
        q, k, v, mixed, mixed_other, lse, w_all, fours, cot_a, cot_b = gate(
            q, k, v, mixed, mixed_other, lse, w_all, fours, cot_a, cot_b
        )
        out_mine, mixed_other = gate(out_mine, mixed_other)
        out_other = core_swap(out_mine)
        dense_pieces = [out_mine, out_other] + twos + fours + twos_swapped + [core_swap(four) for four in fours]
    other = core_swap(mixed_other)

    blank = jnp.zeros((width,), BF16)
    vec = jnp.stack(
        [out_bias, first_gain, first_shift, down_bias, second_gain, second_shift, blank, blank]
    ).astype(F32)
    (
        layer_a, layer_b, gm_mine, gm_other, active, middle_low, grad_branch, grad_upper, grad_attn, grad_one, sums,
    ) = dense(
        place, dense_pieces, x_mine, mixed, other, cot_a, cot_b, vec, up_bias_rel.reshape(1, nt * units), 256
    )
    gm_got = core_swap(gm_other)
    home_0 = lax.ppermute(layer_a, BOTH, column(0, 0, True))

    def total_of(parts):
        total = parts[0].astype(F32)
        for part in parts[1:]:
            total = total + part.astype(F32)
        return total

    class Plane:
        def __init__(self, first, keep, send, got=None):
            self.first, self.got = first, got
            self.keep = self.split(keep)
            self.send = send if isinstance(send, list) else self.split(send)

        def split(self, x):
            return [x[: self.first], x[self.first :]]

        def first_sends(self):
            if self.got is None:
                return self.send
            got = self.split(self.got)
            self.keep = [[keep, g[:, :2]] for keep, g in zip(self.keep, got)]
            return [total_of([send, g[:, 2:]]).astype(BF16) for send, g in zip(self.send, got)]

        def first_moves(self, sends):
            return [chip_step(sends[0], 1), chip_step(sends[1], 2)]

        def second_sends(self, moves):
            keep = [k if isinstance(k, list) else [k] for k in self.keep]
            own = [total_of([part[:, 0] for part in k] + [m[:, 0]]) for k, m in zip(keep, moves)]
            sends = [total_of([part[:, 1] for part in k] + [m[:, 1]]).astype(BF16) for k, m in zip(keep, moves)]
            return own, sends

        def second_moves(self, sends):
            return [chip_step(sends[0], 2), chip_step(sends[1], 1)]

        def sums(self, own, moves):
            return [total_of([o, m]) for o, m in zip(own, moves)]

    class SlowPlane(Plane):
        def __init__(self, first, keep, send, got=None):
            self.first, self.view = first, keep if got is None else keep + got.astype(F32)

        def first_sends(self):
            return []

        def first_moves(self, sends):
            return []

        def second_sends(self, moves):
            return [], []

        def second_moves(self, sends):
            return []

        def sums(self, own, moves):
            pick = lambda step: lax.dynamic_index_in_dim(self.view, chip ^ step, 0, keepdims=False)
            total = total_of([pick(0)] + [chip_step(pick(step).astype(BF16), step) for step in range(1, chips)])
            return self.split(total.transpose(1, 0, 2))

    fast = chips == 4 and aligned

    def grads_of(left, right, extra, first):
        if fast:
            return weight_grad(place, left, right, extra, drows, first)
        grads = mm_lt(left, right)
        if extra:
            near, far = mm_lt(extra[0], extra[1]), mm_lt(extra[0], extra[2])
            head = [jnp.where(core == 0, near, far), jnp.where(core == 0, far, near)]
            grads = jnp.concatenate(head + [grads], axis=1)
        view = grads.reshape(chips, 2, drows, grads.shape[1] // width, width)
        ours = lax.dynamic_index_in_dim(view, core, 1, keepdims=False)
        theirs = lax.dynamic_index_in_dim(view, 1 - core, 1, keepdims=False).astype(BF16)
        return ours, theirs, theirs

    plane_of = Plane if fast else SlowPlane
    down_keep, down_send, down_theirs = grads_of(grad_branch, active, [], 2)
    down_got = core_swap(down_theirs)
    middle_low, down_keep, down_send, down_theirs, gm_got = gate(
        middle_low, down_keep, down_send, down_theirs, gm_got
    )
    up_keep, up_send, up_theirs = grads_of(middle_low, grad_upper, [grad_attn, mixed, other], 3)
    up_keep, up_send, up_theirs, home_0 = gate(up_keep, up_send, up_theirs, home_0)
    up_got = core_swap(up_theirs)

    down = plane_of(2, down_keep, down_send, down_got)
    d_sends = down.first_sends()
    pairs_0, gm_got, d_sends, layer_b = gate(pair_slots, gm_got, d_sends, layer_b)
    d_moves = down.first_moves(d_sends)
    home_1 = lax.ppermute(layer_b, BOTH, column(1, 0, True))
    packed_0, sums_0 = attend_back(pairs_0, 0, q, k, v, gm_mine, gm_got, seg_row, seg_col, lse, hs)
    packed_0, sums_0, d_moves, up_got, home_1 = gate(packed_0, sums_0, d_moves, up_got, home_1)
    layer_out = at_home(home_0, home_1)
    d_own, d_sends = down.second_sends(d_moves)
    up = plane_of(3, up_keep, up_send, up_got)
    u_sends = up.first_sends()
    pairs_1, d_own, d_sends, u_sends = gate(pair_slots, d_own, d_sends, u_sends)
    d_moves = down.second_moves(d_sends)
    u_moves = up.first_moves(u_sends)
    packed_1, sums_1 = attend_back(pairs_1, 1, q, k, v, gm_mine, gm_got, seg_row, seg_col, lse, hs)
    packed_1, sums_1, d_moves = gate(packed_1, sums_1, d_moves)
    d_first, d_second = down.sums(d_own, d_moves)
    d_second = d_second.astype(BF16)
    pair_slots, packed_1, d_first, d_second = gate(pair_slots, packed_1, d_first, d_second)
    d_second = z_step(d_second, 2)
    packed_2, sums_2 = attend_back(pair_slots, 2, q, k, v, gm_mine, gm_got, seg_row, seg_col, lse, hs)
    packed_2, sums_2, u_moves, d_second = gate(packed_2, sums_2, u_moves, d_second)
    d_keep = total_of([d_first[0], d_second[0]])
    d_give = total_of([d_first[1], d_second[1]]).astype(BF16)
    u_own, u_sends = up.second_sends(u_moves)

    head_sums = jnp.concatenate([part[row] for row in range(2) for part in (sums_0, sums_1, sums_2)])[None]
    blank = jnp.zeros_like(head_sums)
    sums = jnp.concatenate(
        [
            sums[:12],
            jnp.where(core == 0, head_sums, blank),
            jnp.where(core == 0, blank, head_sums),
            jnp.zeros((2, width), F32),
        ]
    )
    packed_2, d_keep, d_give, u_own, u_sends, sums = gate(packed_2, d_keep, d_give, u_own, u_sends, sums)
    packed = [packed_0, packed_1, packed_2]
    d_give = z_step(d_give, 1)
    sums_got = z_step(sums, 1)
    u_moves = up.second_moves(u_sends)
    in_mine, in_other = in_grad(packed, w_all, grad_one)
    in_mine, in_other, sums_got, packed, d_give, u_moves = gate(
        in_mine, in_other, sums_got, packed, d_give, u_moves
    )
    in_got = core_swap(in_other)
    down_grad = (d_keep + d_give.astype(F32)).T
    sums = sums + sums_got
    u_first, u_second = up.sums(u_own, u_moves)
    out_near = jnp.where(half == 0, u_first[0, :, :cols], u_first[0, :, cols:])
    out_far = jnp.where(half == 0, u_first[0, :, cols:], u_first[0, :, :cols])
    u_first = u_first[1:]
    u_second = jnp.concatenate([u_second[0], u_second[1], out_far], axis=1).astype(BF16)
    packed, sums, u_first, u_second, out_near = gate(packed, sums, u_first, u_second, out_near)
    u_second = z_step(u_second, 2)
    sums_got = z_step(sums, 2)
    if fast:
        qkv_keep, *qkv_send = qkv_grads(place, x_parts, packed, 2 * drows)
    else:
        parts = [mm_lt(jnp.concatenate(x_parts), packed[g]).reshape(chips, 2 * drows, 3 * lanes) for g in (0, 2, 1)]
        qkv_keep = qkv_send = jnp.stack(parts, axis=2)
    qkv_keep, qkv_send, packed, in_got, sums_got, u_second = gate(
        qkv_keep, qkv_send, packed, in_got, sums_got, u_second
    )
    sums = sums + sums_got
    qkv = plane_of(2, qkv_keep, qkv_send)
    a_sends = qkv.first_sends()
    u_keep, u_give = [total_of([u_first[j], u_second[:, units * j : units * (j + 1)]]) for j in range(2)]
    out_near = total_of([out_near, u_second[:, 2 * units :]])

    def out_unit(wanted_low):
        parts = [
            jnp.concatenate(
                [out_near[:, lanes * w : lanes * (w + 1)], out_near[:, 2 * lanes + hs * w : 2 * lanes + hs * (w + 1)]],
                axis=1,
            )
            for w in range(2)
        ]
        return jnp.where(wanted_low == 0, parts[0], parts[1])

    u_give = jnp.concatenate([u_give, out_unit(1 - low)], axis=1).astype(BF16)
    out_near = out_unit(low)
    a_moves = qkv.second_moves(a_sends)
    in_low = [total_of([part[rows * k : rows * (k + 1)] for part in (in_mine, in_got)]).astype(BF16) for k in range(2)]
    in_low, a_sends, sums, u_keep, u_give, out_near = gate(in_low, a_sends, sums, u_keep, u_give, out_near)
    homes = [lax.ppermute(part, BOTH, column(k, 0, True)) for k, part in enumerate(in_low)]
    a_moves = qkv.first_moves(a_sends)
    u_give = z_step(u_give, 1)
    a_own, a_sends = qkv.second_sends(a_moves)
    a_moves = qkv.second_moves(a_sends)
    up_grad = total_of([u_keep, u_give[:, :units]])
    out_grad = total_of([out_near, u_give[:, units:]]).T.reshape(lheads, hs, drows)
    homes, a_moves, sums = gate(homes, a_moves, sums)
    sums = sums + core_swap(sums)
    for bit in range(chips.bit_length() - 1):
        sums = sums + chip_step(sums, 1 << bit)
    outb_grad, gain_one_grad, shift_one_grad, downb_grad, gain_two_grad, shift_two_grad = [
        sums[row] for row in range(6)
    ]
    upb_grad = lax.dynamic_index_in_dim(sums, 8 + tensor, 0, keepdims=False)
    head_row = jnp.where(half == 0, sums[12], sums[13]).reshape(2, 6, hs)
    qvb_grad = jnp.where(low == 0, head_row[:, [0, 1, 4]], head_row[:, [2, 3, 5]])
    qvb_grad = jnp.concatenate([qvb_grad[0], qvb_grad[1]], axis=1)

    input_grad = at_home(*homes)
    sum_a, sum_b = qkv.sums(a_own, a_moves)
    sum_0, sum_2, sum_1 = [part.reshape(2, drows, 3 * lanes) for part in (sum_a[0], sum_a[1], sum_b[0])]
    sum_01 = [sum_0, sum_1]

    def share(c, u):
        third = [sum_2[c][:, lanes * k + hs * u : lanes * k + hs * (u + 1)] for k in range(3)]
        return jnp.concatenate([sum_01[u][c]] + third, axis=1)

    shares = [[share(c, u).astype(BF16) for u in range(2)] for c in range(2)]
    qkv_grad = jnp.zeros((drows, 3 * lheads * hs), F32)
    for flip in range(2):
        for step in range(2):
            by_core = [jnp.where((low ^ step) == 0, shares[c][0], shares[c][1]) for c in range(2)]
            sent = jnp.where((half ^ flip) == 0, by_core[0], by_core[1])
            qkv_grad = qkv_grad + lax.ppermute(sent, BOTH, column(step, flip, False)).astype(F32)
    pairs_part = qkv_grad[:, : 3 * lanes].reshape(drows, 3, 2, hs)
    third_part = qkv_grad[:, 3 * lanes :].reshape(drows, 3, 1, hs)
    qkv_grad = jnp.concatenate([pairs_part, third_part], axis=2).transpose(0, 2, 1, 3)
    qkv_grad = qkv_grad.reshape(drows, lheads, 3 * hs)
    return (
        layer_out,
        input_grad,
        qkv_grad,
        qvb_grad,
        out_grad,
        outb_grad,
        gain_one_grad,
        shift_one_grad,
        up_grad,
        upb_grad,
        down_grad,
        downb_grad,
        gain_two_grad,
        shift_two_grad,
    )


def solution(mesh):
    return jax.shard_map(
        per_device,
        mesh=mesh,
        in_specs=(
            P("dp", "tensor", None),
            P("dp", None),
            P("tensor", None),
            P("dp", "tensor", None),
            P("tensor", None),
            P("tensor", None, "dp"),
            P(),
            P(),
            P(),
            P("dp", "tensor"),
            P("tensor"),
            P("tensor", "dp"),
            P(),
            P(),
            P(),
            P("dp", "tensor", None),
        ),
        out_specs=(
            P("dp", "tensor", None),
            P("dp", "tensor", None),
            P("dp", "tensor", None),
            P("tensor", None),
            P("tensor", None, "dp"),
            P(),
            P(),
            P(),
            P("dp", "tensor"),
            P("tensor"),
            P("tensor", "dp"),
            P(),
            P(),
            P(),
        ),
        check_vma=False,
    )
```

profile of v0, /device:TPU:0, one launch (start us, length us, event | category | flops | bytes accessed | tf_op | source)
XLA Modules:
  0.0 382.7 jit_solution(10604081992528141744)
XLA Ops:
  5.3 3.1 collective-permute-start
  8.4 2.6 collective-permute-start.1
  11.0 3.8 %collective-permute-done = bf16[104,768]{1,0:T(8,128)(2,1)S(1)} collective-permute-done((bf16[104,768]{1,0:T(8,128)(2,1)S(1)}, bf16[104,768]{1,0:T(8,128)(2,1)S(1)}, u32[]{:S(2)}, u32[]{:S(2)}) %collective-permute-start) | collective-permute-done | bytes 159776 | tf_op jit(solution)/shard_map/ppermute | solution.py:688
  14.9 8.3 %collective-permute-done.1 = bf16[104,768]{1,0:T(8,128)(2,1)S(1)} collective-permute-done((bf16[104,768]{1,0:T(8,128)(2,1)S(1)}, bf16[104,768]{1,0:T(8,128)(2,1)S(1)}, u32[]{:S(2)}, u32[]{:S(2)}) %collective-permute-start.1) | collective-permute-done | bytes 159776 | tf_op jit(solution)/shard_map/ppermute | solution.py:688
  27.4 5.1 %collective-permute-done.4 = bf16[96,1536]{1,0:T(8,128)(2,1)S(1)} collective-permute-done((bf16[96,1536]{1,0:T(8,128)(2,1)S(1)}, bf16[96,1536]{1,0:T(8,128)(2,1)S(1)}, u32[]{:S(2)}, u32[]{:S(2)}) %collective-permute-start.4) | collective-permute-done | bytes 294944 | tf_op jit(solution)/shard_map/ppermute | solution.py:688
  42.2 19.3 %collective-permute-done.9 = bf16[2,96,1536]{2,1,0:T(8,128)(2,1)S(1)} collective-permute-done((bf16[2,96,1536]{2,1,0:T(8,128)(2,1)S(1)}, bf16[2,96,1536]{2,1,0:T(8,128)(2,1)S(1)}, u32[]{:S(2)}, u32[]{:S(2)}) %collective-permute-start.9) | collective-permute-done | bytes 589856 | tf_op jit(solution)/shard_map/ppermute | solution.py:765
  61.7 3.3 collective-permute-done.6.refs_4_
  66.6 4.8 %collective-permute-start.13 = (bf16[512,768]{1,0:T(8,128)(2,1)}, bf16[512,768]{1,0:T(8,128)(2,1)}, u32[]{:S(2)}, u32[]{:S(2)}) collective-permute-start(bf16[512,768]{1,0:T(8,128)(2,1)} %get-tuple-element.381), channel_id=1, source_target_pairs={{0,1},{1,0},{2,5},{3,4},{4,3},{5,2},{6,7},{7,6},{8,9},{9,8},{10,13... | collective-permute-start | bytes 2359304 | tf_op jit(solution)/shard_map/ppermute | solution.py:708
  77.2 7.6 %collective-permute-done.11 = bf16[2,96,1536]{2,1,0:T(8,128)(2,1)} collective-permute-done((bf16[2,96,1536]{2,1,0:T(8,128)(2,1)S(1)}, bf16[2,96,1536]{2,1,0:T(8,128)(2,1)}, u32[]{:S(2)}, u32[]{:S(2)}) %collective-permute-start.11) | collective-permute-done | bytes 589856 | tf_op jit(solution)/shard_map/ppermute | solution.py:691
  87.0 3.1 collective-permute-done.13
  103.6 29.5 %attend.1 = (bf16[2048,384]{1,0:T(8,128)(2,1)}, bf16[2048,384]{1,0:T(8,128)(2,1)}, bf16[2048,384]{1,0:T(8,128)(2,1)}, bf16[1024,384]{1,0:T(8,128)(2,1)}, bf16[10...) custom-call(s32[6,4]{1,0:T(8,128)} %pad_add_fusion.1.pair_ref, s32[2]{0:T(128)} %pad_add_fusion.2.place_ref, ...), custom_call_target="tpu_custom_call" | custom-call | flops 1000000000 | bytes 65536 | tf_op jit(solution)/shard_map/attend/pallas_call | solution.py:126
  133.2 2.7 collective-permute-start.23
  139.7 2.6 collective-permute-done.22.refs_1_
  147.2 43.2 %dense.1 = (bf16[512,768]{1,0:T(8,128)(2,1)S(1)}, bf16[512,768]{1,0:T(8,128)(2,1)S(1)}, bf16[1024,384]{1,0:T(8,128)(2,1)S(1)}, bf16[1024,384]{1,0:T(8,128)(2,1)S...) custom-call(s32[2]{0:T(128)S(1)} %copy-done.32, ...), custom_call_target="tpu_custom_call" | custom-call | flops 1000000000 | bytes 65536 | tf_op jit(solution)/shard_map/dense/pallas_call | solution.py:537
  193.1 2.8 copy-done.6
  195.9 7.8 %weight_grad.2 = (f32[4,2,96,768]{3,2,1,0:T(8,128)S(1)}, bf16[4,2,96,768]{3,2,1,0:T(8,128)(2,1)S(1)}, bf16[4,4,96,768]{3,2,1,0:T(8,128)(2,1)S(1)}) custom-call(s32[2]{0:T(128)S(1)} %copy-done.32, bf16[1024,768]{1,0:T(8,128)(2,1)S(1)} %get-tuple-element.216.refs_0_, bf16[1024,3072]{1,0:T(8,128)(2,1)S(1)} %copy-done.6), custom_call_target="tpu_custom_call" | custom-call | flops 1000000000 | bytes 65536 | tf_op jit(solution)/shard_map/weight_grad/pallas_call | solution.py:616
  203.7 6.9 %collective-permute-start.28 = (bf16[4,4,96,768]{3,2,1,0:T(8,128)(2,1)S(1)}, bf16[4,4,96,768]{3,2,1,0:T(8,128)(2,1)S(1)}, u32[]{:S(2)}, u32[]{:S(2)}) collective-permute-start(bf16[4,4,96,768]{3,2,1,0:T(8,128)(2,1)S(1)} %get-tuple-element.220), channel_id=1, source_target_pairs={{0,4},{4,0},{8,12},{12,8},{16,20},{20,16},{24,28},{28,24},{1,5},{5... | collective-permute-start | bytes 7077896 | tf_op jit(solution)/shard_map/ppermute | solution.py:685
  210.6 9.6 %weight_grad.3 = (f32[5,2,96,768]{3,2,1,0:T(8,128)S(1)}, bf16[5,2,96,768]{3,2,1,0:T(8,128)(2,1)S(1)}, bf16[5,4,96,768]{3,2,1,0:T(8,128)(2,1)S(1)}) custom-call(s32[2]{0:T(128)S(1)} %copy-done.32, bf16[1024,768]{1,0:T(8,128)(2,1)S(1)} %get-tuple-element.222.refs_0_, bf16[1024,3072]{1,0:T(8,128)(2,1)S(1)} %copy-done.7, ...), custom_call_target="tpu_custom_call" | custom-call | flops 1000000000 | bytes 65536 | tf_op jit(solution)/shard_map/weight_grad/pallas_call | solution.py:616
  223.2 10.7 %attend_back.3 = (bf16[2048,384]{1,0:T(8,128)(2,1)S(1)}, f32[8,128]{1,0:T(8,128)S(1)}) custom-call(s32[6,4]{1,0:T(8,128)S(1)} %copy-done.31, s32[1]{0:T(128)} %constant.127.clone.1.group_ref, bf16[2048,384]{1,0:T(8,128)(2,1)S(1)} %copy-done.3, bf16[2048,384]{1,0:T(8,128)(2,1)S(1)} %copy-done.4, bf16[2048,384]{1,0:T(8,128)(2,1)S(1)} %copy-done.5, ...), custom_call_target="tpu_custom_call" | custom-call | flops 1000000000 | bytes 65536 | tf_op jit(solution)/shard_map/attend_back/pallas_call | solution.py:224
  233.9 2.8 collective-permute-done.29
  238.0 3.7 collective-permute-done.32
  247.4 10.9 %attend_back.4 = (bf16[2048,384]{1,0:T(8,128)(2,1)S(1)}, f32[8,128]{1,0:T(8,128)S(1)}) custom-call(s32[6,4]{1,0:T(8,128)S(1)} %copy-done.31, s32[1]{0:T(128)} %constant.128.clone.1.group_ref, bf16[2048,384]{1,0:T(8,128)(2,1)S(1)} %copy-done.3, bf16[2048,384]{1,0:T(8,128)(2,1)S(1)} %copy-done.4, bf16[2048,384]{1,0:T(8,128)(2,1)S(1)} %copy-done.5, ...), custom_call_target="tpu_custom_call" | custom-call | flops 1000000000 | bytes 65536 | tf_op jit(solution)/shard_map/attend_back/pallas_call | solution.py:224
  258.6 10.7 %attend_back.5 = (bf16[2048,384]{1,0:T(8,128)(2,1)S(1)}, f32[8,128]{1,0:T(8,128)S(1)}) custom-call(s32[6,4]{1,0:T(8,128)S(1)} %copy-done.31, s32[1]{0:T(128)} %constant.129.clone.1.group_ref, bf16[2048,384]{1,0:T(8,128)(2,1)S(1)} %copy-done.3, bf16[2048,384]{1,0:T(8,128)(2,1)S(1)} %copy-done.4, bf16[2048,384]{1,0:T(8,128)(2,1)S(1)} %copy-done.5, ...), custom_call_target="tpu_custom_call" | custom-call | flops 1000000000 | bytes 65536 | tf_op jit(solution)/shard_map/attend_back/pallas_call | solution.py:224
  284.0 6.0 %in_grad.1 = (f32[1024,768]{1,0:T(8,128)S(1)}, bf16[1024,768]{1,0:T(8,128)(2,1)S(1)}) custom-call(bf16[2048,384]{1,0:T(8,128)(2,1)S(1)} %get-tuple-element.298.refs_0_, bf16[2048,384]{1,0:T(8,128)(2,1)S(1)} %copy-done.9, bf16[2048,384]{1,0:T(8,128)(2,1)S(1)} %copy-done.12, bf16[3,768,384]{2,1,0:T(8,128)(2,1)S(1)} %copy-done.21, f32[1024,768]{1,0:T(8,128)S(1)} %copy-done.20), custom_call_target="tpu_custom_call" | custom-call | flops 1000000000 | bytes 65536 | tf_op jit(solution)/shard_map/in_grad/pallas_call | solution.py:351
  296.3 6.7 %qkv_grads.1 = (f32[3,2,192,384]{3,2,1,0:T(8,128)S(1)}, bf16[2,2,192,384]{3,2,1,0:T(8,128)(2,1)S(1)}, bf16[1,2,192,384]{3,2,1,0:T(8,128)(2,1)S(1)}) custom-call(s32[2]{0:T(128)S(1)} %copy-done.32, bf16[2048,384]{1,0:T(8,128)(2,1)S(1)} %get-tuple-element.298.refs_0_, bf16[2048,384]{1,0:T(8,128)(2,1)S(1)} %copy-done.10, bf16[2048,384]{1,0:T(8,128)(2,1)S(1)} %copy-done.13, ...), custom_call_target="tpu_custom_call" | custom-call | flops 1000000000 | bytes 65536 | tf_op jit(solution)/shard_map/qkv_grads/pallas_call | solution.py:301
  304.2 10.5 %collective-permute-done.43 = f32[16,768]{1,0:T(8,128)S(1)} collective-permute-done((f32[16,768]{1,0:T(8,128)S(1)}, f32[16,768]{1,0:T(8,128)S(1)}, u32[]{:S(2)}, u32[]{:S(2)}) %collective-permute-start.43) | collective-permute-done | bytes 49184 | tf_op jit(solution)/shard_map/ppermute | solution.py:688
  321.9 7.4 %collective-permute-start.45 = (bf16[512,768]{1,0:T(8,128)(2,1)}, bf16[512,768]{1,0:T(8,128)(2,1)}, u32[]{:S(2)}, u32[]{:S(2)}) collective-permute-start(bf16[512,768]{1,0:T(8,128)(2,1)} %get-tuple-element.314), channel_id=1, source_target_pairs={{0,0},{1,1},{4,2},{5,3},{2,4},{3,5},{6,6},{7,7},{8,8},{9,9},{12,10... | collective-permute-start | bytes 2359304 | tf_op jit(solution)/shard_map/ppermute | solution.py:1015
  337.9 3.3 collective-permute-done.50
  341.1 16.8 %collective-permute-done.46 = bf16[512,768]{1,0:T(8,128)(2,1)} collective-permute-done((bf16[512,768]{1,0:T(8,128)(2,1)S(1)}, bf16[512,768]{1,0:T(8,128)(2,1)}, u32[]{:S(2)}, u32[]{:S(2)}) %collective-permute-start.46) | collective-permute-done | bytes 786464 | tf_op jit(solution)/shard_map/ppermute | solution.py:1015
  361.6 4.3 %collective-permute-start.52 = (bf16[96,576]{1,0:T(8,128)(2,1)S(1)}, bf16[96,576]{1,0:T(8,128)(2,1)S(1)}, u32[]{:S(2)}, u32[]{:S(2)}) collective-permute-start(bf16[96,576]{1,0:T(8,128)(2,1)S(1)} %broadcast_select_fusion.16), channel_id=1, source_target_pairs={{0,1},{1,0},{2,5},{3,4},{4,3},{5,2},{6,7},{7,6},{8,9},{9,8},{10,13... | collective-permute-start | bytes 331784 | tf_op jit(solution)/shard_map/ppermute | solution.py:1049
  365.9 3.3 collective-permute-start.53
  375.6 2.8 collective-permute-done.53
  (411 shorter events, 113.9 us)
Async XLA Ops:
  8.4 14.8 %collective-permute-start.1 = (bf16[104,768]{1,0:T(8,128)(2,1)S(1)}, bf16[104,768]{1,0:T(8,128)(2,1)S(1)}, u32[]{:S(2)}, u32[]{:S(2)}) collective-permute-start(bf16[104,768]{1,0:T(8,128)(2,1)S(1)} %pad_maximum_fusion.11), channel_id=1, source_target_pairs={{0,2},{1,3},{2,0},{3,1},{4,6},{5,7},{6,4},{7,5},{8,10},{9,11},{10,... | collective-permute-start | bytes 479240 | tf_op jit(solution)/shard_map/ppermute | solution.py:688
  35.5 26.1 %collective-permute-start.5 = (bf16[4,192,384]{2,1,0:T(8,128)(2,1)S(1)}, bf16[4,192,384]{2,1,0:T(8,128)(2,1)S(1)}, u32[]{:S(2)}, u32[]{:S(2)}) collective-permute-start(bf16[4,192,384]{2,1,0:T(8,128)(2,1)S(1)} %maximum_select_fusion.refs_2_), channel_id=1, source_target_pairs={{0,8},{4,12},{8,0},{12,4},{16,24},{20,28},{24,16},{28,20},{1,9},{5... | collective-permute-start | bytes 1769480 | tf_op jit(solution)/shard_map/ppermute | solution.py:691
  37.1 28.0 %collective-permute-start.6 = (bf16[4,192,384]{2,1,0:T(8,128)(2,1)S(1)}, bf16[4,192,384]{2,1,0:T(8,128)(2,1)S(1)}, u32[]{:S(2)}, u32[]{:S(2)}) collective-permute-start(bf16[4,192,384]{2,1,0:T(8,128)(2,1)S(1)} %maximum_select_fusion.refs_2_), channel_id=1, source_target_pairs={{0,16},{4,20},{8,24},{12,28},{16,0},{20,4},{24,8},{28,12},{1,17},{... | collective-permute-start | bytes 1769480 | tf_op jit(solution)/shard_map/ppermute | solution.py:691
  38.6 26.4 %collective-permute-start.7 = (bf16[4,192,384]{2,1,0:T(8,128)(2,1)S(1)}, bf16[4,192,384]{2,1,0:T(8,128)(2,1)S(1)}, u32[]{:S(2)}, u32[]{:S(2)}) collective-permute-start(bf16[4,192,384]{2,1,0:T(8,128)(2,1)S(1)} %maximum_select_fusion.refs_2_), channel_id=1, source_target_pairs={{0,24},{4,28},{8,16},{12,20},{16,8},{20,12},{24,0},{28,4},{1,25},{... | collective-permute-start | bytes 1769480 | tf_op jit(solution)/shard_map/ppermute | solution.py:691
  39.1 22.5 %collective-permute-start.9 = (bf16[2,96,1536]{2,1,0:T(8,128)(2,1)S(1)}, bf16[2,96,1536]{2,1,0:T(8,128)(2,1)S(1)}, u32[]{:S(2)}, u32[]{:S(2)}) collective-permute-start(bf16[2,96,1536]{2,1,0:T(8,128)(2,1)S(1)} %collective-permute-done.8), channel_id=1, source_target_pairs={{1,0},{2,3},{5,4},{6,7},{9,8},{10,11},{13,12},{14,15},{17,16},{18,... | collective-permute-start | bytes 1769480 | tf_op jit(solution)/shard_map/ppermute | solution.py:765
  41.4 23.7 %collective-permute-start.10 = (bf16[512,768]{1,0:T(8,128)(2,1)S(1)}, bf16[512,768]{1,0:T(8,128)(2,1)S(1)}, u32[]{:S(2)}, u32[]{:S(2)}) collective-permute-start(bf16[512,768]{1,0:T(8,128)(2,1)S(1)} %get-tuple-element.382), channel_id=1, source_target_pairs={{0,0},{1,1},{2,4},{3,5},{4,2},{5,3},{6,6},{7,7},{8,8},{9,9},{10,12... | collective-permute-start | bytes 2359304 | tf_op jit(solution)/shard_map/ppermute | solution.py:708
  66.6 23.5 %collective-permute-start.13 = (bf16[512,768]{1,0:T(8,128)(2,1)}, bf16[512,768]{1,0:T(8,128)(2,1)}, u32[]{:S(2)}, u32[]{:S(2)}) collective-permute-start(bf16[512,768]{1,0:T(8,128)(2,1)} %get-tuple-element.381), channel_id=1, source_target_pairs={{0,1},{1,0},{2,5},{3,4},{4,3},{5,2},{6,7},{7,6},{8,9},{9,8},{10,13... | collective-permute-start | bytes 2359304 | tf_op jit(solution)/shard_map/ppermute | solution.py:708
  92.6 40.6 %collective-permute-start.18 = (bf16[2,2,96,1536]{3,2,1,0:T(8,128)(2,1)}, bf16[2,2,96,1536]{3,2,1,0:T(8,128)(2,1)}, u32[]{:S(2)}, u32[]{:S(2)}) collective-permute-start(bf16[2,2,96,1536]{3,2,1,0:T(8,128)(2,1)} %pad_maximum_fusion.2.refs_2_), channel_id=1, source_target_pairs={{0,16},{4,20},{8,24},{12,28},{16,0},{20,4},{24,8},{28,12},{1,17},{... | collective-permute-start | bytes 3538952 | tf_op jit(solution)/shard_map/ppermute | solution.py:691
  93.1 40.1 %collective-permute-start.19 = (bf16[2,2,96,1536]{3,2,1,0:T(8,128)(2,1)}, bf16[2,2,96,1536]{3,2,1,0:T(8,128)(2,1)}, u32[]{:S(2)}, u32[]{:S(2)}) collective-permute-start(bf16[2,2,96,1536]{3,2,1,0:T(8,128)(2,1)} %pad_maximum_fusion.3.refs_3_), channel_id=1, source_target_pairs={{0,8},{4,12},{8,0},{12,4},{16,24},{20,28},{24,16},{28,20},{1,9},{5... | collective-permute-start | bytes 3538952 | tf_op jit(solution)/shard_map/ppermute | solution.py:691
  98.6 34.6 %collective-permute-start.20 = (bf16[512,768]{1,0:T(8,128)(2,1)}, bf16[512,768]{1,0:T(8,128)(2,1)S(1)}, u32[]{:S(2)}, u32[]{:S(2)}) collective-permute-start(bf16[512,768]{1,0:T(8,128)(2,1)} %get-tuple-element.203), channel_id=1, source_target_pairs={{0,0},{1,1},{2,4},{3,5},{4,2},{5,3},{6,6},{7,7},{8,8},{9,9},{10,12... | collective-permute-start | bytes 2359304 | tf_op jit(solution)/shard_map/ppermute | solution.py:708
  100.4 32.8 %collective-permute-start.21 = (bf16[512,768]{1,0:T(8,128)(2,1)}, bf16[512,768]{1,0:T(8,128)(2,1)S(1)}, u32[]{:S(2)}, u32[]{:S(2)}) collective-permute-start(bf16[512,768]{1,0:T(8,128)(2,1)} %get-tuple-element.204), channel_id=1, source_target_pairs={{0,1},{1,0},{2,5},{3,4},{4,3},{5,2},{6,7},{7,6},{8,9},{9,8},{10,13... | collective-permute-start | bytes 2359304 | tf_op jit(solution)/shard_map/ppermute | solution.py:708
  192.0 18.6 %collective-permute-start.26 = (bf16[1024,384]{1,0:T(8,128)(2,1)S(1)}, bf16[1024,384]{1,0:T(8,128)(2,1)S(1)}, u32[]{:S(2)}, u32[]{:S(2)}) collective-permute-start(bf16[1024,384]{1,0:T(8,128)(2,1)S(1)} %get-tuple-element.221), channel_id=1, source_target_pairs={{0,4},{4,0},{8,12},{12,8},{16,20},{20,16},{24,28},{28,24},{1,5},{5... | collective-permute-start | bytes 2359304 | tf_op jit(solution)/shard_map/ppermute | solution.py:685
  192.4 27.8 %collective-permute-start.27 = (bf16[512,768]{1,0:T(8,128)(2,1)S(1)}, bf16[512,768]{1,0:T(8,128)(2,1)S(1)}, u32[]{:S(2)}, u32[]{:S(2)}) collective-permute-start(bf16[512,768]{1,0:T(8,128)(2,1)S(1)} %get-tuple-element.228), channel_id=1, source_target_pairs={{0,0},{1,1},{4,2},{5,3},{2,4},{3,5},{6,6},{7,7},{8,8},{9,9},{12,10... | collective-permute-start | bytes 2359304 | tf_op jit(solution)/shard_map/ppermute | solution.py:845
  203.7 16.6 %collective-permute-start.28 = (bf16[4,4,96,768]{3,2,1,0:T(8,128)(2,1)S(1)}, bf16[4,4,96,768]{3,2,1,0:T(8,128)(2,1)S(1)}, u32[]{:S(2)}, u32[]{:S(2)}) collective-permute-start(bf16[4,4,96,768]{3,2,1,0:T(8,128)(2,1)S(1)} %get-tuple-element.220), channel_id=1, source_target_pairs={{0,4},{4,0},{8,12},{12,8},{16,20},{20,16},{24,28},{28,24},{1,5},{5... | collective-permute-start | bytes 7077896 | tf_op jit(solution)/shard_map/ppermute | solution.py:685
  220.2 21.4 %collective-permute-start.31 = (bf16[5,4,96,768]{3,2,1,0:T(8,128)(2,1)S(1)}, bf16[5,4,96,768]{3,2,1,0:T(8,128)(2,1)S(1)}, u32[]{:S(2)}, u32[]{:S(2)}) collective-permute-start(bf16[5,4,96,768]{3,2,1,0:T(8,128)(2,1)S(1)} %get-tuple-element.244), channel_id=1, source_target_pairs={{0,4},{4,0},{8,12},{12,8},{16,20},{20,16},{24,28},{28,24},{1,5},{5... | collective-permute-start | bytes 8847368 | tf_op jit(solution)/shard_map/ppermute | solution.py:685
  221.2 20.4 %collective-permute-start.32 = (bf16[512,768]{1,0:T(8,128)(2,1)S(1)}, bf16[512,768]{1,0:T(8,128)(2,1)S(1)}, u32[]{:S(2)}, u32[]{:S(2)}) collective-permute-start(bf16[512,768]{1,0:T(8,128)(2,1)S(1)} %get-tuple-element.245), channel_id=1, source_target_pairs={{1,0},{0,1},{5,2},{4,3},{3,4},{2,5},{7,6},{6,7},{9,8},{8,9},{13,10... | collective-permute-start | bytes 2359304 | tf_op jit(solution)/shard_map/ppermute | solution.py:934
  221.2 15.5 %collective-permute-start.29 = (bf16[2,2,96,768]{3,2,0,1:T(8,128)(2,1)S(1)}, bf16[2,2,96,768]{3,2,0,1:T(8,128)(2,1)S(1)}, u32[]{:S(2)}, u32[]{:S(2)}) collective-permute-start(bf16[2,2,96,768]{3,2,0,1:T(8,128)(2,1)S(1)} %get-tuple-element.242), channel_id=1, source_target_pairs={{0,8},{4,12},{8,0},{12,4},{16,24},{20,28},{24,16},{28,20},{1,9},{5... | collective-permute-start | bytes 1769480 | tf_op jit(solution)/shard_map/ppermute | solution.py:691
  221.8 16.2 %collective-permute-start.30 = (bf16[2,2,96,768]{3,2,0,1:T(8,128)(2,1)S(1)}, bf16[2,2,96,768]{3,2,0,1:T(8,128)(2,1)S(1)}, u32[]{:S(2)}, u32[]{:S(2)}) collective-permute-start(bf16[2,2,96,768]{3,2,0,1:T(8,128)(2,1)S(1)} %get-tuple-element.243), channel_id=1, source_target_pairs={{0,16},{4,20},{8,24},{12,28},{16,0},{20,4},{24,8},{28,12},{1,17},{... | collective-permute-start | bytes 1769480 | tf_op jit(solution)/shard_map/ppermute | solution.py:691
  243.3 15.1 %collective-permute-start.33 = (bf16[2,96,768]{2,1,0:T(8,128)(2,1)S(1)}, bf16[2,96,768]{2,1,0:T(8,128)(2,1)S(1)}, u32[]{:S(2)}, u32[]{:S(2)}) collective-permute-start(bf16[2,96,768]{2,1,0:T(8,128)(2,1)S(1)} %get-tuple-element.256), channel_id=1, source_target_pairs={{0,16},{4,20},{8,24},{12,28},{16,0},{20,4},{24,8},{28,12},{1,17},{... | collective-permute-start | bytes 884744 | tf_op jit(solution)/shard_map/ppermute | solution.py:691
  243.3 15.0 %collective-permute-start.34 = (bf16[2,96,768]{2,1,0:T(8,128)(2,1)S(1)}, bf16[2,96,768]{2,1,0:T(8,128)(2,1)S(1)}, u32[]{:S(2)}, u32[]{:S(2)}) collective-permute-start(bf16[2,96,768]{2,1,0:T(8,128)(2,1)S(1)} %fusion.18), channel_id=1, source_target_pairs={{0,8},{4,12},{8,0},{12,4},{16,24},{20,28},{24,16},{28,20},{1,9},{5... | collective-permute-start | bytes 884744 | tf_op jit(solution)/shard_map/ppermute | solution.py:691
  245.0 25.1 %collective-permute-start.35 = (bf16[3,2,96,768]{3,2,0,1:T(8,128)(2,1)S(1)}, bf16[3,2,96,768]{3,2,0,1:T(8,128)(2,1)S(1)}, u32[]{:S(2)}, u32[]{:S(2)}) collective-permute-start(bf16[3,2,96,768]{3,2,0,1:T(8,128)(2,1)S(1)} %add_convert_fusion), channel_id=1, source_target_pairs={{0,8},{4,12},{8,0},{12,4},{16,24},{20,28},{24,16},{28,20},{1,9},{5... | collective-permute-start | bytes 2654216 | tf_op jit(solution)/shard_map/ppermute | solution.py:691
  245.4 24.3 %collective-permute-start.36 = (bf16[2,2,96,768]{3,2,0,1:T(8,128)(2,1)S(1)}, bf16[2,2,96,768]{3,2,0,1:T(8,128)(2,1)S(1)}, u32[]{:S(2)}, u32[]{:S(2)}) collective-permute-start(bf16[2,2,96,768]{3,2,0,1:T(8,128)(2,1)S(1)} %add_convert_fusion.3), channel_id=1, source_target_pairs={{0,16},{4,20},{8,24},{12,28},{16,0},{20,4},{24,8},{28,12},{1,17},{... | collective-permute-start | bytes 1769480 | tf_op jit(solution)/shard_map/ppermute | solution.py:691
  273.4 16.7 %collective-permute-start.40 = (bf16[3,96,768]{2,1,0:T(8,128)(2,1)}, bf16[3,96,768]{2,1,0:T(8,128)(2,1)}, u32[]{:S(2)}, u32[]{:S(2)}) collective-permute-start(bf16[3,96,768]{2,1,0:T(8,128)(2,1)} %get-tuple-element.287), channel_id=1, source_target_pairs={{0,16},{4,20},{8,24},{12,28},{16,0},{20,4},{24,8},{28,12},{1,17},{... | collective-permute-start | bytes 1327112 | tf_op jit(solution)/shard_map/ppermute | solution.py:691
  275.1 15.0 %collective-permute-start.41 = (bf16[2,96,768]{2,1,0:T(8,128)(2,1)S(1)}, bf16[2,96,768]{2,1,0:T(8,128)(2,1)}, u32[]{:S(2)}, u32[]{:S(2)}) collective-permute-start(bf16[2,96,768]{2,1,0:T(8,128)(2,1)S(1)} %fusion.19), channel_id=1, source_target_pairs={{0,8},{4,12},{8,0},{12,4},{16,24},{20,28},{24,16},{28,20},{1,9},{5... | collective-permute-start | bytes 884744 | tf_op jit(solution)/shard_map/ppermute | solution.py:691
  291.3 23.3 %collective-permute-start.42 = (bf16[1024,768]{1,0:T(8,128)(2,1)S(1)}, bf16[1024,768]{1,0:T(8,128)(2,1)S(1)}, u32[]{:S(2)}, u32[]{:S(2)}) collective-permute-start(bf16[1024,768]{1,0:T(8,128)(2,1)S(1)} %get-tuple-element.304), channel_id=1, source_target_pairs={{0,4},{4,0},{8,12},{12,8},{16,20},{20,16},{24,28},{28,24},{1,5},{5... | collective-permute-start | bytes 4718600 | tf_op jit(solution)/shard_map/ppermute | solution.py:685
  293.0 21.7 %collective-permute-start.44 = (bf16[96,1920]{1,0:T(8,128)(2,1)S(1)}, bf16[96,1920]{1,0:T(8,128)(2,1)S(1)}, u32[]{:S(2)}, u32[]{:S(2)}) collective-permute-start(bf16[96,1920]{1,0:T(8,128)(2,1)S(1)} %pad_maximum_fusion.6), channel_id=1, source_target_pairs={{0,2},{1,3},{2,0},{3,1},{4,6},{5,7},{6,4},{7,5},{8,10},{9,11},{10,... | collective-permute-start | bytes 1105928 | tf_op jit(solution)/shard_map/ppermute | solution.py:688
  295.2 19.5 %collective-permute-start.43 = (f32[16,768]{1,0:T(8,128)S(1)}, f32[16,768]{1,0:T(8,128)S(1)}, u32[]{:S(2)}, u32[]{:S(2)}) collective-permute-start(f32[16,768]{1,0:T(8,128)S(1)} %add.284), channel_id=1, source_target_pairs={{0,2},{1,3},{2,0},{3,1},{4,6},{5,7},{6,4},{7,5},{8,10},{9,11},{10,... | collective-permute-start | bytes 147464 | tf_op jit(solution)/shard_map/ppermute | solution.py:688
  317.1 15.6 %collective-permute-start.47 = (bf16[2,2,192,384]{3,2,0,1:T(8,128)(2,1)}, bf16[2,2,192,384]{3,2,0,1:T(8,128)(2,1)}, u32[]{:S(2)}, u32[]{:S(2)}) collective-permute-start(bf16[2,2,192,384]{3,2,0,1:T(8,128)(2,1)} %copy.94), channel_id=1, source_target_pairs={{0,8},{4,12},{8,0},{12,4},{16,24},{20,28},{24,16},{28,20},{1,9},{5... | collective-permute-start | bytes 1769480 | tf_op jit(solution)/shard_map/ppermute | solution.py:691
  321.9 19.3 %collective-permute-start.45 = (bf16[512,768]{1,0:T(8,128)(2,1)}, bf16[512,768]{1,0:T(8,128)(2,1)}, u32[]{:S(2)}, u32[]{:S(2)}) collective-permute-start(bf16[512,768]{1,0:T(8,128)(2,1)} %get-tuple-element.314), channel_id=1, source_target_pairs={{0,0},{1,1},{4,2},{5,3},{2,4},{3,5},{6,6},{7,7},{8,8},{9,9},{12,10... | collective-permute-start | bytes 2359304 | tf_op jit(solution)/shard_map/ppermute | solution.py:1015
  329.3 28.6 %collective-permute-start.46 = (bf16[512,768]{1,0:T(8,128)(2,1)S(1)}, bf16[512,768]{1,0:T(8,128)(2,1)}, u32[]{:S(2)}, u32[]{:S(2)}) collective-permute-start(bf16[512,768]{1,0:T(8,128)(2,1)S(1)} %get-tuple-element.315), channel_id=1, source_target_pairs={{1,0},{0,1},{5,2},{4,3},{3,4},{2,5},{7,6},{6,7},{9,8},{8,9},{13,10... | collective-permute-start | bytes 2359304 | tf_op jit(solution)/shard_map/ppermute | solution.py:1015
  333.8 24.1 %collective-permute-start.48 = (bf16[2,192,384]{2,1,0:T(8,128)(2,1)S(1)}, bf16[2,192,384]{2,1,0:T(8,128)(2,1)S(1)}, u32[]{:S(2)}, u32[]{:S(2)}) collective-permute-start(bf16[2,192,384]{2,1,0:T(8,128)(2,1)S(1)} %fusion.21), channel_id=1, source_target_pairs={{0,16},{4,20},{8,24},{12,28},{16,0},{20,4},{24,8},{28,12},{1,17},{... | collective-permute-start | bytes 884744 | tf_op jit(solution)/shard_map/ppermute | solution.py:691
  360.9 14.7 %collective-permute-start.51 = (bf16[96,576]{1,0:T(8,128)(2,1)S(1)}, bf16[96,576]{1,0:T(8,128)(2,1)S(1)}, u32[]{:S(2)}, u32[]{:S(2)}) collective-permute-start(bf16[96,576]{1,0:T(8,128)(2,1)S(1)} %broadcast_select_fusion.17), channel_id=1, source_target_pairs={{0,0},{1,1},{2,4},{3,5},{4,2},{5,3},{6,6},{7,7},{8,8},{9,9},{10,12... | collective-permute-start | bytes 331784 | tf_op jit(solution)/shard_map/ppermute | solution.py:1049
  (98 other events, 888.5 us)
where the time goes:
time: 390 us; the launch traced here: 383 us
  Pallas kernels  135 us (35%)
  waiting for transfers between devices  103 us (26%)
  starting transfers between devices  76.6 us (20%)
  local copies, waits for them, and re-layouts  36.2 us (9%)
  other arithmetic  29.2 us (7%)
    pallas_call x1, Pallas kernels, dense(): pl.pallas_call(functools.partial(dense_kernel, n_w=len(w_pieces), chunks=...  43.2 us
    pallas_call x3, Pallas kernels, attend_back(): pl.pallas_call(functools.partial(attend_back_kernel, rows=rows, hs=hs, bl...  32.4 us
    pallas_call x1, Pallas kernels, attend(): pl.pallas_call(functools.partial(attend_kernel, rows=rows, hs=hs, blocks=...  29.5 us
    ppermute x10, waiting for transfers between devices, z_step(): return lax.ppermute(x, 'tensor', [(i, i ^ k) for i in range(nt)])  28 us
    ppermute x21, waiting for transfers between devices, chip_step(): return lax.ppermute(x, 'dp', [(i, i ^ 2 * k) for i in range(ndp)])  22.1 us
    unnamed x142, local copies, waits for them, and re-layouts  21.8 us
    ppermute x21, starting transfers between devices, chip_step(): return lax.ppermute(x, 'dp', [(i, i ^ 2 * k) for i in range(ndp)])  21.4 us
    ppermute x1, waiting for transfers between devices, per_device(): ff_end = lax.ppermute(ff_middle, 'tensor', [(1, 0), (2, 3)])  19.3 us
  transfers between devices with their start and end apart: 59, of which 21 were waited for; matrix products, arithmetic and copies ran while one was open for 7% of the time, Pallas kernels for 24%

commit v1 on v0

--- a/solution.py
+++ b/solution.py
@@ -361,7 +361,7 @@
             jax.ShapeDtypeStruct((seq // 2, width), F32),
             jax.ShapeDtypeStruct((seq // 2, width), BF16),
         ],
-        compiler_params=pltpu.CompilerParams(vmem_limit_bytes=12 << 20),
+        compiler_params=pltpu.CompilerParams(vmem_limit_bytes=58 << 20),
         cost_estimate=COST,
         name="in_grad",
     )(*packed, weight, extra)
@@ -562,7 +562,7 @@
             ],
         ),
         out_shape=[jax.ShapeDtypeStruct(*s) for s in shapes],
-        compiler_params=pltpu.CompilerParams(vmem_limit_bytes=27 << 20),
+        compiler_params=pltpu.CompilerParams(vmem_limit_bytes=58 << 20),
         cost_estimate=COST,
         name="dense",
     )(place, *w_pieces, x, mine, other, cot_a, cot_b, vec, upb)
@@ -933,8 +933,7 @@
     d_moves = down.first_moves(d_sends)
     home_1 = lax.ppermute(layer_b, BOTH, column(1, 0, True))
     packed_0, sums_0 = attend_back(pairs_0, 0, q, k, v, gm_mine, gm_got, seg_row, seg_col, lse, hs)
-    packed_0, sums_0, d_moves, up_got, home_1 = gate(packed_0, sums_0, d_moves, up_got, home_1)
-    layer_out = at_home(home_0, home_1)
+    packed_0, sums_0, d_moves, up_got = gate(packed_0, sums_0, d_moves, up_got)
     d_own, d_sends = down.second_sends(d_moves)
     up = plane_of(3, up_keep, up_send, up_got)
     u_sends = up.first_sends()
@@ -942,7 +941,8 @@
     d_moves = down.second_moves(d_sends)
     u_moves = up.first_moves(u_sends)
     packed_1, sums_1 = attend_back(pairs_1, 1, q, k, v, gm_mine, gm_got, seg_row, seg_col, lse, hs)
-    packed_1, sums_1, d_moves = gate(packed_1, sums_1, d_moves)
+    packed_1, sums_1, d_moves, home_1 = gate(packed_1, sums_1, d_moves, home_1)
+    layer_out = at_home(home_0, home_1)
     d_first, d_second = down.sums(d_own, d_moves)
     d_second = d_second.astype(BF16)
     pair_slots, packed_1, d_first, d_second = gate(pair_slots, packed_1, d_first, d_second)
@@ -980,20 +980,21 @@
     out_far = jnp.where(half == 0, u_first[0, :, cols:], u_first[0, :, :cols])
     u_first = u_first[1:]
     u_second = jnp.concatenate([u_second[0], u_second[1], out_far], axis=1).astype(BF16)
-    packed, sums, u_first, u_second, out_near = gate(packed, sums, u_first, u_second, out_near)
+    in_got, sums, u_first, u_second, out_near = gate(in_got, sums, u_first, u_second, out_near)
     u_second = z_step(u_second, 2)
     sums_got = z_step(sums, 2)
+    in_low = [total_of([part[rows * k : rows * (k + 1)] for part in (in_mine, in_got)]).astype(BF16) for k in range(2)]
+    packed, in_low = gate(packed, in_low)
+    homes = [lax.ppermute(part, BOTH, column(k, 0, True)) for k, part in enumerate(in_low)]
     if fast:
         qkv_keep, *qkv_send = qkv_grads(place, x_parts, packed, 2 * drows)
     else:
         parts = [mm_lt(jnp.concatenate(x_parts), packed[g]).reshape(chips, 2 * drows, 3 * lanes) for g in (0, 2, 1)]
         qkv_keep = qkv_send = jnp.stack(parts, axis=2)
-    qkv_keep, qkv_send, packed, in_got, sums_got, u_second = gate(
-        qkv_keep, qkv_send, packed, in_got, sums_got, u_second
-    )
+    qkv_keep, qkv_send, u_second, sums_got = gate(qkv_keep, qkv_send, u_second, sums_got)
     sums = sums + sums_got
     qkv = plane_of(2, qkv_keep, qkv_send)
-    a_sends = qkv.first_sends()
+    a_moves = qkv.first_moves(qkv.first_sends())
     u_keep, u_give = [total_of([u_first[j], u_second[:, units * j : units * (j + 1)]]) for j in range(2)]
     out_near = total_of([out_near, u_second[:, 2 * units :]])
 
@@ -1009,11 +1010,6 @@
 
     u_give = jnp.concatenate([u_give, out_unit(1 - low)], axis=1).astype(BF16)
     out_near = out_unit(low)
-    a_moves = qkv.second_moves(a_sends)
-    in_low = [total_of([part[rows * k : rows * (k + 1)] for part in (in_mine, in_got)]).astype(BF16) for k in range(2)]
-    in_low, a_sends, sums, u_keep, u_give, out_near = gate(in_low, a_sends, sums, u_keep, u_give, out_near)
-    homes = [lax.ppermute(part, BOTH, column(k, 0, True)) for k, part in enumerate(in_low)]
-    a_moves = qkv.first_moves(a_sends)
     u_give = z_step(u_give, 1)
     a_own, a_sends = qkv.second_sends(a_moves)
     a_moves = qkv.second_moves(a_sends)

time: 390 us -> 380 us (0.974)
  waiting for transfers between devices: 103 us -> 88 us
  local copies, waits for them, and re-layouts: 36.2 us -> 25.3 us
  Pallas kernels: 135 us -> 143 us
  starting transfers between devices: 76.6 us -> 84.5 us
    ppermute x2, waiting for transfers between devices: 16.8 us -> 2.03 us  [per_device(): lax.ppermute(part, BOTH, column(k, 0, True))]
    unnamed x142 -> x136, local copies, waits for them, and re-layouts: 21.8 us -> 12 us
    ppermute x14, starting transfers between devices: 12.2 us -> 18.9 us  [core_swap(): return lax.ppermute(x, 'dp', core_pairs)]
    ppermute x2, starting transfers between devices: 9.45 us -> 3.79 us  [per_device(): lax.ppermute(part, BOTH, column(k, 0, True))]
    ppermute x4, starting transfers between devices: 8.36 us -> 13.2 us  [per_device(): lax.ppermute(sent, BOTH, column(step, flip, False)).astype(F32)]
    pallas_call x1, Pallas kernels: 6.05 us -> 10.3 us  [in_grad(): pl.pallas_call(functools.partial(in_grad_kernel, n=n, half=half), grid=(2...]
  transfers between devices with their start and end apart: 59 -> 59, of which waited for: 21 -> 22; matrix products, arithmetic and copies ran while one was open for 7% -> 8% of each run, Pallas kernels for 24% -> 26%
where the time goes in v1:
time: 380 us; the launch traced here: 373 us
  Pallas kernels  143 us (38%)
  waiting for transfers between devices  88 us (23%)
  starting transfers between devices  84.5 us (22%)
  other arithmetic  29.3 us (8%)
  local copies, waits for them, and re-layouts  25.3 us (7%)
    pallas_call x1, Pallas kernels, dense(): pl.pallas_call(functools.partial(dense_kernel, n_w=len(w_pieces), chunks=...  46.7 us
    pallas_call x3, Pallas kernels, attend_back(): pl.pallas_call(functools.partial(attend_back_kernel, rows=rows, hs=hs, bl...  32.4 us
    pallas_call x1, Pallas kernels, attend(): pl.pallas_call(functools.partial(attend_kernel, rows=rows, hs=hs, blocks=...  29.5 us
    ppermute x10, waiting for transfers between devices, z_step(): return lax.ppermute(x, 'tensor', [(i, i ^ k) for i in range(nt)])  29 us
    ppermute x21, waiting for transfers between devices, chip_step(): return lax.ppermute(x, 'dp', [(i, i ^ 2 * k) for i in range(ndp)])  24.7 us
    ppermute x21, starting transfers between devices, chip_step(): return lax.ppermute(x, 'dp', [(i, i ^ 2 * k) for i in range(ndp)])  22.6 us
    ppermute x1, waiting for transfers between devices, per_device(): ff_end = lax.ppermute(ff_middle, 'tensor', [(1, 0), (2, 3)])  19.4 us
    ppermute x14, starting transfers between devices, core_swap(): return lax.ppermute(x, 'dp', core_pairs)  18.9 us
  transfers between devices with their start and end apart: 59, of which 22 were waited for; matrix products, arithmetic and copies ran while one was open for 8% of the time, Pallas kernels for 26%

profile of v1, /device:TPU:0, one launch (start us, length us, event | category | flops | bytes accessed | tf_op | source)
XLA Modules:
  0.0 372.9 jit_solution(6070970956817899583)
XLA Ops:
  5.3 3.1 collective-permute-start
  8.4 2.6 collective-permute-start.1
  11.0 3.8 %collective-permute-done = bf16[104,768]{1,0:T(8,128)(2,1)S(1)} collective-permute-done((bf16[104,768]{1,0:T(8,128)(2,1)S(1)}, bf16[104,768]{1,0:T(8,128)(2,1)S(1)}, u32[]{:S(2)}, u32[]{:S(2)}) %collective-permute-start) | collective-permute-done | bytes 159776 | tf_op jit(solution)/shard_map/ppermute | solution.py:688
  14.9 8.3 %collective-permute-done.1 = bf16[104,768]{1,0:T(8,128)(2,1)S(1)} collective-permute-done((bf16[104,768]{1,0:T(8,128)(2,1)S(1)}, bf16[104,768]{1,0:T(8,128)(2,1)S(1)}, u32[]{:S(2)}, u32[]{:S(2)}) %collective-permute-start.1) | collective-permute-done | bytes 159776 | tf_op jit(solution)/shard_map/ppermute | solution.py:688
  24.0 2.4 collective-permute-start.4
  27.1 5.1 %collective-permute-done.4 = bf16[96,1536]{1,0:T(8,128)(2,1)S(1)} collective-permute-done((bf16[96,1536]{1,0:T(8,128)(2,1)S(1)}, bf16[96,1536]{1,0:T(8,128)(2,1)S(1)}, u32[]{:S(2)}, u32[]{:S(2)}) %collective-permute-start.4) | collective-permute-done | bytes 294944 | tf_op jit(solution)/shard_map/ppermute | solution.py:688
  41.8 19.4 %collective-permute-done.9 = bf16[2,96,1536]{2,1,0:T(8,128)(2,1)S(1)} collective-permute-done((bf16[2,96,1536]{2,1,0:T(8,128)(2,1)S(1)}, bf16[2,96,1536]{2,1,0:T(8,128)(2,1)S(1)}, u32[]{:S(2)}, u32[]{:S(2)}) %collective-permute-start.9) | collective-permute-done | bytes 589856 | tf_op jit(solution)/shard_map/ppermute | solution.py:765
  61.4 3.3 collective-permute-done.6.refs_4_
  66.4 4.8 %collective-permute-start.13 = (bf16[512,768]{1,0:T(8,128)(2,1)}, bf16[512,768]{1,0:T(8,128)(2,1)S(1)}, u32[]{:S(2)}, u32[]{:S(2)}) collective-permute-start(bf16[512,768]{1,0:T(8,128)(2,1)} %get-tuple-element.369), channel_id=1, source_target_pairs={{0,1},{1,0},{2,5},{3,4},{4,3},{5,2},{6,7},{7,6},{8,9},{9,8},{10,13... | collective-permute-start | bytes 2359304 | tf_op jit(solution)/shard_map/ppermute | solution.py:708
  76.1 2.3 pad_maximum_fusion.3.refs_3_
  78.4 6.2 %collective-permute-done.11 = bf16[2,96,1536]{2,1,0:T(8,128)(2,1)} collective-permute-done((bf16[2,96,1536]{2,1,0:T(8,128)(2,1)S(1)}, bf16[2,96,1536]{2,1,0:T(8,128)(2,1)}, u32[]{:S(2)}, u32[]{:S(2)}) %collective-permute-start.11) | collective-permute-done | bytes 589856 | tf_op jit(solution)/shard_map/ppermute | solution.py:691
  86.8 3.0 collective-permute-done.13
  92.8 2.6 collective-permute-done.15.refs_6_
  102.0 29.5 %attend.1 = (bf16[2048,384]{1,0:T(8,128)(2,1)}, bf16[2048,384]{1,0:T(8,128)(2,1)}, bf16[2048,384]{1,0:T(8,128)(2,1)}, bf16[1024,384]{1,0:T(8,128)(2,1)}, bf16[10...) custom-call(s32[6,4]{1,0:T(8,128)} %pad_add_fusion.1.pair_ref, s32[2]{0:T(128)} %pad_add_fusion.2.place_ref, ...), custom_call_target="tpu_custom_call" | custom-call | flops 1000000000 | bytes 65536 | tf_op jit(solution)/shard_map/attend/pallas_call | solution.py:126
  131.7 2.7 collective-permute-start.23
  138.0 2.2 collective-permute-done.22.refs_1_
  142.0 46.7 %dense.1 = (bf16[512,768]{1,0:T(8,128)(2,1)}, bf16[512,768]{1,0:T(8,128)(2,1)}, bf16[1024,384]{1,0:T(8,128)(2,1)}, bf16[1024,384]{1,0:T(8,128)(2,1)}, bf16[1024,...) custom-call(s32[2]{0:T(128)} %pad_add_fusion.2.place_ref, ...), custom_call_target="tpu_custom_call" | custom-call | flops 1000000000 | bytes 65536 | tf_op jit(solution)/shard_map/dense/pallas_call | solution.py:537
  191.0 2.8 copy-done.7
  195.2 7.8 %weight_grad.2 = (f32[4,2,96,768]{3,2,1,0:T(8,128)S(1)}, bf16[4,2,96,768]{3,2,1,0:T(8,128)(2,1)S(1)}, bf16[4,4,96,768]{3,2,1,0:T(8,128)(2,1)S(1)}) custom-call(s32[2]{0:T(128)S(1)} %copy-done.27, bf16[1024,768]{1,0:T(8,128)(2,1)S(1)} %copy-done.23, bf16[1024,3072]{1,0:T(8,128)(2,1)S(1)} %copy-done.7), custom_call_target="tpu_custom_call" | custom-call | flops 1000000000 | bytes 65536 | tf_op jit(solution)/shard_map/weight_grad/pallas_call | solution.py:616
  203.0 5.9 %collective-permute-start.28 = (bf16[4,4,96,768]{3,2,1,0:T(8,128)(2,1)S(1)}, bf16[4,4,96,768]{3,2,1,0:T(8,128)(2,1)S(1)}, u32[]{:S(2)}, u32[]{:S(2)}) collective-permute-start(bf16[4,4,96,768]{3,2,1,0:T(8,128)(2,1)S(1)} %get-tuple-element.214), channel_id=1, source_target_pairs={{0,4},{4,0},{8,12},{12,8},{16,20},{20,16},{24,28},{28,24},{1,5},{5... | collective-permute-start | bytes 7077896 | tf_op jit(solution)/shard_map/ppermute | solution.py:685
  211.8 9.6 %weight_grad.3 = (f32[5,2,96,768]{3,2,1,0:T(8,128)S(1)}, bf16[5,2,96,768]{3,2,1,0:T(8,128)(2,1)S(1)}, bf16[5,4,96,768]{3,2,1,0:T(8,128)(2,1)S(1)}) custom-call(s32[2]{0:T(128)S(1)} %copy-done.27, bf16[1024,768]{1,0:T(8,128)(2,1)S(1)} %copy-done.21, bf16[1024,3072]{1,0:T(8,128)(2,1)S(1)} %copy-done.8, bf16[1024,768]{1,0:T(8,128)(2,1)S(1)} %copy-done.22, ...), custom_call_target="tpu_custom_call" | custom-call | flops 1000000000 | bytes 65536 | tf_op jit(solution)/shard_map/weight_grad/pallas_call | solution.py:616
  224.2 10.7 %attend_back.3 = (bf16[2048,384]{1,0:T(8,128)(2,1)S(1)}, f32[8,128]{1,0:T(8,128)S(1)}) custom-call(s32[6,4]{1,0:T(8,128)S(1)} %copy-done.26, s32[1]{0:T(128)} %constant.127.clone.1.group_ref, bf16[2048,384]{1,0:T(8,128)(2,1)S(1)} %copy-done.3, bf16[2048,384]{1,0:T(8,128)(2,1)S(1)} %copy-done.4, bf16[2048,384]{1,0:T(8,128)(2,1)S(1)} %copy-done.5, ...), custom_call_target="tpu_custom_call" | custom-call | flops 1000000000 | bytes 65536 | tf_op jit(solution)/shard_map/attend_back/pallas_call | solution.py:224
  234.9 2.8 collective-permute-done.29
  242.9 11.0 %attend_back.4 = (bf16[2048,384]{1,0:T(8,128)(2,1)S(1)}, f32[8,128]{1,0:T(8,128)S(1)}) custom-call(s32[6,4]{1,0:T(8,128)S(1)} %copy-done.26, s32[1]{0:T(128)} %constant.128.clone.1.group_ref, bf16[2048,384]{1,0:T(8,128)(2,1)S(1)} %copy-done.3, bf16[2048,384]{1,0:T(8,128)(2,1)S(1)} %copy-done.4, bf16[2048,384]{1,0:T(8,128)(2,1)S(1)} %copy-done.5, ...), custom_call_target="tpu_custom_call" | custom-call | flops 1000000000 | bytes 65536 | tf_op jit(solution)/shard_map/attend_back/pallas_call | solution.py:224
  254.2 10.7 %attend_back.5 = (bf16[2048,384]{1,0:T(8,128)(2,1)S(1)}, f32[8,128]{1,0:T(8,128)S(1)}) custom-call(s32[6,4]{1,0:T(8,128)S(1)} %copy-done.26, s32[1]{0:T(128)} %constant.129.clone.1.group_ref, bf16[2048,384]{1,0:T(8,128)(2,1)S(1)} %copy-done.3, bf16[2048,384]{1,0:T(8,128)(2,1)S(1)} %copy-done.4, bf16[2048,384]{1,0:T(8,128)(2,1)S(1)} %copy-done.5, ...), custom_call_target="tpu_custom_call" | custom-call | flops 1000000000 | bytes 65536 | tf_op jit(solution)/shard_map/attend_back/pallas_call | solution.py:224
  274.1 10.3 %in_grad.1 = (f32[1024,768]{1,0:T(8,128)}, bf16[1024,768]{1,0:T(8,128)(2,1)}) custom-call(bf16[2048,384]{1,0:T(8,128)(2,1)} %copy-done.9, bf16[2048,384]{1,0:T(8,128)(2,1)} %copy-done.11, bf16[2048,384]{1,0:T(8,128)(2,1)} %copy-done.13, bf16[3,768,384]{2,1,0:T(8,128)(2,1)} %get-tuple-element.275.refs_3_, f32[1024,768]{1,0:T(8,128)} %get-tuple-element.276.refs_4_), custom_call_target="tpu_custom_call" | custom-call | flops 1000000000 | bytes 65536 | tf_op jit(solution)/shard_map/in_grad/pallas_call | solution.py:351
  292.7 6.7 %qkv_grads.1 = (f32[3,2,192,384]{3,2,1,0:T(8,128)S(1)}, bf16[2,2,192,384]{3,2,1,0:T(8,128)(2,1)S(1)}, bf16[1,2,192,384]{3,2,1,0:T(8,128)(2,1)S(1)}) custom-call(s32[2]{0:T(128)S(1)} %copy-done.27, bf16[2048,384]{1,0:T(8,128)(2,1)S(1)} %copy-done.10, bf16[2048,384]{1,0:T(8,128)(2,1)S(1)} %copy-done.12, bf16[2048,384]{1,0:T(8,128)(2,1)S(1)} %copy-done.14, ...), custom_call_target="tpu_custom_call" | custom-call | flops 1000000000 | bytes 65536 | tf_op jit(solution)/shard_map/qkv_grads/pallas_call | solution.py:301
  299.5 9.8 %collective-permute-done.46 = f32[16,768]{1,0:T(8,128)S(1)} collective-permute-done((f32[16,768]{1,0:T(8,128)S(1)}, f32[16,768]{1,0:T(8,128)S(1)}, u32[]{:S(2)}, u32[]{:S(2)}) %collective-permute-start.46) | collective-permute-done | bytes 49184 | tf_op jit(solution)/shard_map/ppermute | solution.py:688
  319.1 6.8 %collective-permute-done.47 = bf16[2,2,192,384]{3,2,0,1:T(8,128)(2,1)} collective-permute-done((bf16[2,2,192,384]{3,2,0,1:T(8,128)(2,1)}, bf16[2,2,192,384]{3,2,0,1:T(8,128)(2,1)}, u32[]{:S(2)}, u32[]{:S(2)}) %collective-permute-start.47) | collective-permute-done | bytes 589856 | tf_op jit(solution)/shard_map/ppermute | solution.py:691
  338.1 8.1 %collective-permute-start.55 = (f32[16,768]{1,0:T(8,128)S(1)}, f32[16,768]{1,0:T(8,128)S(1)}, u32[]{:S(2)}, u32[]{:S(2)}) collective-permute-start(f32[16,768]{1,0:T(8,128)S(1)} %copy-done.44), channel_id=1, source_target_pairs={{0,4},{4,0},{8,12},{12,8},{16,20},{20,16},{24,28},{28,24},{1,5},{5... | collective-permute-start | bytes 147464 | tf_op jit(solution)/shard_map/ppermute | solution.py:685
  346.9 9.2 %collective-permute-start.52 = (bf16[96,576]{1,0:T(8,128)(2,1)S(1)}, bf16[96,576]{1,0:T(8,128)(2,1)S(1)}, u32[]{:S(2)}, u32[]{:S(2)}) collective-permute-start(bf16[96,576]{1,0:T(8,128)(2,1)S(1)} %broadcast_select_fusion.16), channel_id=1, source_target_pairs={{0,1},{1,0},{2,5},{3,4},{4,3},{5,2},{6,7},{7,6},{8,9},{9,8},{10,13... | collective-permute-start | bytes 331784 | tf_op jit(solution)/shard_map/ppermute | solution.py:1045
  356.0 3.3 collective-permute-start.53
  (403 shorter events, 106.6 us)
Async XLA Ops:
  8.4 14.8 %collective-permute-start.1 = (bf16[104,768]{1,0:T(8,128)(2,1)S(1)}, bf16[104,768]{1,0:T(8,128)(2,1)S(1)}, u32[]{:S(2)}, u32[]{:S(2)}) collective-permute-start(bf16[104,768]{1,0:T(8,128)(2,1)S(1)} %pad_maximum_fusion.11), channel_id=1, source_target_pairs={{0,2},{1,3},{2,0},{3,1},{4,6},{5,7},{6,4},{7,5},{8,10},{9,11},{10,... | collective-permute-start | bytes 479240 | tf_op jit(solution)/shard_map/ppermute | solution.py:688
  35.3 26.1 %collective-permute-start.5 = (bf16[4,192,384]{2,1,0:T(8,128)(2,1)S(1)}, bf16[4,192,384]{2,1,0:T(8,128)(2,1)S(1)}, u32[]{:S(2)}, u32[]{:S(2)}) collective-permute-start(bf16[4,192,384]{2,1,0:T(8,128)(2,1)S(1)} %maximum_select_fusion.refs_2_), channel_id=1, source_target_pairs={{0,8},{4,12},{8,0},{12,4},{16,24},{20,28},{24,16},{28,20},{1,9},{5... | collective-permute-start | bytes 1769480 | tf_op jit(solution)/shard_map/ppermute | solution.py:691
  36.8 28.0 %collective-permute-start.6 = (bf16[4,192,384]{2,1,0:T(8,128)(2,1)S(1)}, bf16[4,192,384]{2,1,0:T(8,128)(2,1)S(1)}, u32[]{:S(2)}, u32[]{:S(2)}) collective-permute-start(bf16[4,192,384]{2,1,0:T(8,128)(2,1)S(1)} %maximum_select_fusion.refs_2_), channel_id=1, source_target_pairs={{0,16},{4,20},{8,24},{12,28},{16,0},{20,4},{24,8},{28,12},{1,17},{... | collective-permute-start | bytes 1769480 | tf_op jit(solution)/shard_map/ppermute | solution.py:691
  38.3 26.4 %collective-permute-start.7 = (bf16[4,192,384]{2,1,0:T(8,128)(2,1)S(1)}, bf16[4,192,384]{2,1,0:T(8,128)(2,1)S(1)}, u32[]{:S(2)}, u32[]{:S(2)}) collective-permute-start(bf16[4,192,384]{2,1,0:T(8,128)(2,1)S(1)} %maximum_select_fusion.refs_2_), channel_id=1, source_target_pairs={{0,24},{4,28},{8,16},{12,20},{16,8},{20,12},{24,0},{28,4},{1,25},{... | collective-permute-start | bytes 1769480 | tf_op jit(solution)/shard_map/ppermute | solution.py:691
  38.8 22.4 %collective-permute-start.9 = (bf16[2,96,1536]{2,1,0:T(8,128)(2,1)S(1)}, bf16[2,96,1536]{2,1,0:T(8,128)(2,1)S(1)}, u32[]{:S(2)}, u32[]{:S(2)}) collective-permute-start(bf16[2,96,1536]{2,1,0:T(8,128)(2,1)S(1)} %collective-permute-done.8), channel_id=1, source_target_pairs={{1,0},{2,3},{5,4},{6,7},{9,8},{10,11},{13,12},{14,15},{17,16},{18,... | collective-permute-start | bytes 1769480 | tf_op jit(solution)/shard_map/ppermute | solution.py:765
  41.1 23.7 %collective-permute-start.10 = (bf16[512,768]{1,0:T(8,128)(2,1)S(1)}, bf16[512,768]{1,0:T(8,128)(2,1)S(1)}, u32[]{:S(2)}, u32[]{:S(2)}) collective-permute-start(bf16[512,768]{1,0:T(8,128)(2,1)S(1)} %get-tuple-element.370), channel_id=1, source_target_pairs={{0,0},{1,1},{2,4},{3,5},{4,2},{5,3},{6,6},{7,7},{8,8},{9,9},{10,12... | collective-permute-start | bytes 2359304 | tf_op jit(solution)/shard_map/ppermute | solution.py:708
  66.4 23.4 %collective-permute-start.13 = (bf16[512,768]{1,0:T(8,128)(2,1)}, bf16[512,768]{1,0:T(8,128)(2,1)S(1)}, u32[]{:S(2)}, u32[]{:S(2)}) collective-permute-start(bf16[512,768]{1,0:T(8,128)(2,1)} %get-tuple-element.369), channel_id=1, source_target_pairs={{0,1},{1,0},{2,5},{3,4},{4,3},{5,2},{6,7},{7,6},{8,9},{9,8},{10,13... | collective-permute-start | bytes 2359304 | tf_op jit(solution)/shard_map/ppermute | solution.py:708
  91.1 40.5 %collective-permute-start.18 = (bf16[2,2,96,1536]{3,2,1,0:T(8,128)(2,1)}, bf16[2,2,96,1536]{3,2,1,0:T(8,128)(2,1)}, u32[]{:S(2)}, u32[]{:S(2)}) collective-permute-start(bf16[2,2,96,1536]{3,2,1,0:T(8,128)(2,1)} %pad_maximum_fusion.2.refs_2_), channel_id=1, source_target_pairs={{0,16},{4,20},{8,24},{12,28},{16,0},{20,4},{24,8},{28,12},{1,17},{... | collective-permute-start | bytes 3538952 | tf_op jit(solution)/shard_map/ppermute | solution.py:691
  91.6 40.0 %collective-permute-start.19 = (bf16[2,2,96,1536]{3,2,1,0:T(8,128)(2,1)}, bf16[2,2,96,1536]{3,2,1,0:T(8,128)(2,1)}, u32[]{:S(2)}, u32[]{:S(2)}) collective-permute-start(bf16[2,2,96,1536]{3,2,1,0:T(8,128)(2,1)} %pad_maximum_fusion.3.refs_3_), channel_id=1, source_target_pairs={{0,8},{4,12},{8,0},{12,4},{16,24},{20,28},{24,16},{28,20},{1,9},{5... | collective-permute-start | bytes 3538952 | tf_op jit(solution)/shard_map/ppermute | solution.py:691
  97.1 34.5 %collective-permute-start.20 = (bf16[512,768]{1,0:T(8,128)(2,1)}, bf16[512,768]{1,0:T(8,128)(2,1)S(1)}, u32[]{:S(2)}, u32[]{:S(2)}) collective-permute-start(bf16[512,768]{1,0:T(8,128)(2,1)} %get-tuple-element.197), channel_id=1, source_target_pairs={{0,0},{1,1},{2,4},{3,5},{4,2},{5,3},{6,6},{7,7},{8,8},{9,9},{10,12... | collective-permute-start | bytes 2359304 | tf_op jit(solution)/shard_map/ppermute | solution.py:708
  98.9 32.7 %collective-permute-start.21 = (bf16[512,768]{1,0:T(8,128)(2,1)}, bf16[512,768]{1,0:T(8,128)(2,1)S(1)}, u32[]{:S(2)}, u32[]{:S(2)}) collective-permute-start(bf16[512,768]{1,0:T(8,128)(2,1)} %get-tuple-element.198), channel_id=1, source_target_pairs={{0,1},{1,0},{2,5},{3,4},{4,3},{5,2},{6,7},{7,6},{8,9},{9,8},{10,13... | collective-permute-start | bytes 2359304 | tf_op jit(solution)/shard_map/ppermute | solution.py:708
  188.7 20.2 %collective-permute-start.26 = (bf16[1024,384]{1,0:T(8,128)(2,1)}, bf16[1024,384]{1,0:T(8,128)(2,1)S(1)}, u32[]{:S(2)}, u32[]{:S(2)}) collective-permute-start(bf16[1024,384]{1,0:T(8,128)(2,1)} %get-tuple-element.215), channel_id=1, source_target_pairs={{0,4},{4,0},{8,12},{12,8},{16,20},{20,16},{24,28},{28,24},{1,5},{5... | collective-permute-start | bytes 2359304 | tf_op jit(solution)/shard_map/ppermute | solution.py:685
  189.2 32.2 %collective-permute-start.27 = (bf16[512,768]{1,0:T(8,128)(2,1)}, bf16[512,768]{1,0:T(8,128)(2,1)S(1)}, u32[]{:S(2)}, u32[]{:S(2)}) collective-permute-start(bf16[512,768]{1,0:T(8,128)(2,1)} %get-tuple-element.222), channel_id=1, source_target_pairs={{0,0},{1,1},{4,2},{5,3},{2,4},{3,5},{6,6},{7,7},{8,8},{9,9},{12,10... | collective-permute-start | bytes 2359304 | tf_op jit(solution)/shard_map/ppermute | solution.py:845
  203.0 18.5 %collective-permute-start.28 = (bf16[4,4,96,768]{3,2,1,0:T(8,128)(2,1)S(1)}, bf16[4,4,96,768]{3,2,1,0:T(8,128)(2,1)S(1)}, u32[]{:S(2)}, u32[]{:S(2)}) collective-permute-start(bf16[4,4,96,768]{3,2,1,0:T(8,128)(2,1)S(1)} %get-tuple-element.214), channel_id=1, source_target_pairs={{0,4},{4,0},{8,12},{12,8},{16,20},{20,16},{24,28},{28,24},{1,5},{5... | collective-permute-start | bytes 7077896 | tf_op jit(solution)/shard_map/ppermute | solution.py:685
  221.4 16.6 %collective-permute-start.31 = (bf16[5,4,96,768]{3,2,1,0:T(8,128)(2,1)S(1)}, bf16[5,4,96,768]{3,2,1,0:T(8,128)(2,1)S(1)}, u32[]{:S(2)}, u32[]{:S(2)}) collective-permute-start(bf16[5,4,96,768]{3,2,1,0:T(8,128)(2,1)S(1)} %get-tuple-element.239), channel_id=1, source_target_pairs={{0,4},{4,0},{8,12},{12,8},{16,20},{20,16},{24,28},{28,24},{1,5},{5... | collective-permute-start | bytes 8847368 | tf_op jit(solution)/shard_map/ppermute | solution.py:685
  221.9 15.8 %collective-permute-start.29 = (bf16[2,2,96,768]{3,2,0,1:T(8,128)(2,1)S(1)}, bf16[2,2,96,768]{3,2,0,1:T(8,128)(2,1)S(1)}, u32[]{:S(2)}, u32[]{:S(2)}) collective-permute-start(bf16[2,2,96,768]{3,2,0,1:T(8,128)(2,1)S(1)} %get-tuple-element.237), channel_id=1, source_target_pairs={{0,8},{4,12},{8,0},{12,4},{16,24},{20,28},{24,16},{28,20},{1,9},{5... | collective-permute-start | bytes 1769480 | tf_op jit(solution)/shard_map/ppermute | solution.py:691
  222.6 15.4 %collective-permute-start.30 = (bf16[2,2,96,768]{3,2,0,1:T(8,128)(2,1)S(1)}, bf16[2,2,96,768]{3,2,0,1:T(8,128)(2,1)S(1)}, u32[]{:S(2)}, u32[]{:S(2)}) collective-permute-start(bf16[2,2,96,768]{3,2,0,1:T(8,128)(2,1)S(1)} %get-tuple-element.238), channel_id=1, source_target_pairs={{0,16},{4,20},{8,24},{12,28},{16,0},{20,4},{24,8},{28,12},{1,17},{... | collective-permute-start | bytes 1769480 | tf_op jit(solution)/shard_map/ppermute | solution.py:691
  223.8 30.2 %collective-permute-start.34 = (bf16[512,768]{1,0:T(8,128)(2,1)S(1)}, bf16[512,768]{1,0:T(8,128)(2,1)S(1)}, u32[]{:S(2)}, u32[]{:S(2)}) collective-permute-start(bf16[512,768]{1,0:T(8,128)(2,1)S(1)} %copy-done.60), channel_id=1, source_target_pairs={{1,0},{0,1},{5,2},{4,3},{3,4},{2,5},{7,6},{6,7},{9,8},{8,9},{13,10... | collective-permute-start | bytes 2359304 | tf_op jit(solution)/shard_map/ppermute | solution.py:934
  238.8 15.1 %collective-permute-start.32 = (bf16[2,96,768]{2,1,0:T(8,128)(2,1)S(1)}, bf16[2,96,768]{2,1,0:T(8,128)(2,1)S(1)}, u32[]{:S(2)}, u32[]{:S(2)}) collective-permute-start(bf16[2,96,768]{2,1,0:T(8,128)(2,1)S(1)} %get-tuple-element.247), channel_id=1, source_target_pairs={{0,16},{4,20},{8,24},{12,28},{16,0},{20,4},{24,8},{28,12},{1,17},{... | collective-permute-start | bytes 884744 | tf_op jit(solution)/shard_map/ppermute | solution.py:691
  240.0 14.0 %collective-permute-start.33 = (bf16[2,96,768]{2,1,0:T(8,128)(2,1)S(1)}, bf16[2,96,768]{2,1,0:T(8,128)(2,1)S(1)}, u32[]{:S(2)}, u32[]{:S(2)}) collective-permute-start(bf16[2,96,768]{2,1,0:T(8,128)(2,1)S(1)} %fusion.18), channel_id=1, source_target_pairs={{0,8},{4,12},{8,0},{12,4},{16,24},{20,28},{24,16},{28,20},{1,9},{5... | collective-permute-start | bytes 884744 | tf_op jit(solution)/shard_map/ppermute | solution.py:691
  240.6 26.3 %collective-permute-start.35 = (bf16[3,2,96,768]{3,2,0,1:T(8,128)(2,1)S(1)}, bf16[3,2,96,768]{3,2,0,1:T(8,128)(2,1)S(1)}, u32[]{:S(2)}, u32[]{:S(2)}) collective-permute-start(bf16[3,2,96,768]{3,2,0,1:T(8,128)(2,1)S(1)} %add_convert_fusion), channel_id=1, source_target_pairs={{0,8},{4,12},{8,0},{12,4},{16,24},{20,28},{24,16},{28,20},{1,9},{5... | collective-permute-start | bytes 2654216 | tf_op jit(solution)/shard_map/ppermute | solution.py:691
  242.0 25.0 %collective-permute-start.36 = (bf16[2,2,96,768]{3,2,0,1:T(8,128)(2,1)S(1)}, bf16[2,2,96,768]{3,2,0,1:T(8,128)(2,1)S(1)}, u32[]{:S(2)}, u32[]{:S(2)}) collective-permute-start(bf16[2,2,96,768]{3,2,0,1:T(8,128)(2,1)S(1)} %add_convert_fusion.3), channel_id=1, source_target_pairs={{0,16},{4,20},{8,24},{12,28},{16,0},{20,4},{24,8},{28,12},{1,17},{... | collective-permute-start | bytes 1769480 | tf_op jit(solution)/shard_map/ppermute | solution.py:691
  268.3 16.2 %collective-permute-start.40 = (bf16[3,96,768]{2,1,0:T(8,128)(2,1)S(1)}, bf16[3,96,768]{2,1,0:T(8,128)(2,1)}, u32[]{:S(2)}, u32[]{:S(2)}) collective-permute-start(bf16[3,96,768]{2,1,0:T(8,128)(2,1)S(1)} %get-tuple-element.281), channel_id=1, source_target_pairs={{0,16},{4,20},{8,24},{12,28},{16,0},{20,4},{24,8},{28,12},{1,17},{... | collective-permute-start | bytes 1327112 | tf_op jit(solution)/shard_map/ppermute | solution.py:691
  269.3 15.2 %collective-permute-start.41 = (bf16[2,96,768]{2,1,0:T(8,128)(2,1)S(1)}, bf16[2,96,768]{2,1,0:T(8,128)(2,1)S(1)}, u32[]{:S(2)}, u32[]{:S(2)}) collective-permute-start(bf16[2,96,768]{2,1,0:T(8,128)(2,1)S(1)} %fusion.19), channel_id=1, source_target_pairs={{0,8},{4,12},{8,0},{12,4},{16,24},{20,28},{24,16},{28,20},{1,9},{5... | collective-permute-start | bytes 884744 | tf_op jit(solution)/shard_map/ppermute | solution.py:691
  288.2 21.1 %collective-permute-start.45 = (bf16[96,1920]{1,0:T(8,128)(2,1)S(1)}, bf16[96,1920]{1,0:T(8,128)(2,1)S(1)}, u32[]{:S(2)}, u32[]{:S(2)}) collective-permute-start(bf16[96,1920]{1,0:T(8,128)(2,1)S(1)} %pad_maximum_fusion.6), channel_id=1, source_target_pairs={{0,2},{1,3},{2,0},{3,1},{4,6},{5,7},{6,4},{7,5},{8,10},{9,11},{10,... | collective-permute-start | bytes 1105928 | tf_op jit(solution)/shard_map/ppermute | solution.py:688
  291.0 18.3 %collective-permute-start.46 = (f32[16,768]{1,0:T(8,128)S(1)}, f32[16,768]{1,0:T(8,128)S(1)}, u32[]{:S(2)}, u32[]{:S(2)}) collective-permute-start(f32[16,768]{1,0:T(8,128)S(1)} %add.284), channel_id=1, source_target_pairs={{0,2},{1,3},{2,0},{3,1},{4,6},{5,7},{6,4},{7,5},{8,10},{9,11},{10,... | collective-permute-start | bytes 147464 | tf_op jit(solution)/shard_map/ppermute | solution.py:688
  310.3 15.6 %collective-permute-start.47 = (bf16[2,2,192,384]{3,2,0,1:T(8,128)(2,1)}, bf16[2,2,192,384]{3,2,0,1:T(8,128)(2,1)}, u32[]{:S(2)}, u32[]{:S(2)}) collective-permute-start(bf16[2,2,192,384]{3,2,0,1:T(8,128)(2,1)} %copy.94), channel_id=1, source_target_pairs={{0,8},{4,12},{8,0},{12,4},{16,24},{20,28},{24,16},{28,20},{1,9},{5... | collective-permute-start | bytes 1769480 | tf_op jit(solution)/shard_map/ppermute | solution.py:691
  311.8 20.0 %collective-permute-start.43 = (bf16[512,768]{1,0:T(8,128)(2,1)}, bf16[512,768]{1,0:T(8,128)(2,1)S(1)}, u32[]{:S(2)}, u32[]{:S(2)}) collective-permute-start(bf16[512,768]{1,0:T(8,128)(2,1)} %get-tuple-element.294), channel_id=1, source_target_pairs={{0,0},{1,1},{4,2},{5,3},{2,4},{3,5},{6,6},{7,7},{8,8},{9,9},{12,10... | collective-permute-start | bytes 2359304 | tf_op jit(solution)/shard_map/ppermute | solution.py:988
  313.6 20.2 %collective-permute-start.44 = (bf16[512,768]{1,0:T(8,128)(2,1)}, bf16[512,768]{1,0:T(8,128)(2,1)}, u32[]{:S(2)}, u32[]{:S(2)}) collective-permute-start(bf16[512,768]{1,0:T(8,128)(2,1)} %get-tuple-element.295), channel_id=1, source_target_pairs={{1,0},{0,1},{5,2},{4,3},{3,4},{2,5},{7,6},{6,7},{9,8},{8,9},{13,10... | collective-permute-start | bytes 2359304 | tf_op jit(solution)/shard_map/ppermute | solution.py:988
  338.1 22.5 %collective-permute-start.55 = (f32[16,768]{1,0:T(8,128)S(1)}, f32[16,768]{1,0:T(8,128)S(1)}, u32[]{:S(2)}, u32[]{:S(2)}) collective-permute-start(f32[16,768]{1,0:T(8,128)S(1)} %copy-done.44), channel_id=1, source_target_pairs={{0,4},{4,0},{8,12},{12,8},{16,20},{20,16},{24,28},{28,24},{1,5},{5... | collective-permute-start | bytes 147464 | tf_op jit(solution)/shard_map/ppermute | solution.py:685
  346.2 20.2 %collective-permute-start.51 = (bf16[96,576]{1,0:T(8,128)(2,1)S(1)}, bf16[96,576]{1,0:T(8,128)(2,1)S(1)}, u32[]{:S(2)}, u32[]{:S(2)}) collective-permute-start(bf16[96,576]{1,0:T(8,128)(2,1)S(1)} %broadcast_select_fusion.17), channel_id=1, source_target_pairs={{0,0},{1,1},{2,4},{3,5},{4,2},{5,3},{6,6},{7,7},{8,8},{9,9},{10,12... | collective-permute-start | bytes 331784 | tf_op jit(solution)/shard_map/ppermute | solution.py:1045
  346.9 19.6 %collective-permute-start.52 = (bf16[96,576]{1,0:T(8,128)(2,1)S(1)}, bf16[96,576]{1,0:T(8,128)(2,1)S(1)}, u32[]{:S(2)}, u32[]{:S(2)}) collective-permute-start(bf16[96,576]{1,0:T(8,128)(2,1)S(1)} %broadcast_select_fusion.16), channel_id=1, source_target_pairs={{0,1},{1,0},{2,5},{3,4},{4,3},{5,2},{6,7},{7,6},{8,9},{9,8},{10,13... | collective-permute-start | bytes 331784 | tf_op jit(solution)/shard_map/ppermute | solution.py:1045
  (94 other events, 719.8 us)

commit v2 on v1

--- a/solution.py
+++ b/solution.py
@@ -57,15 +57,18 @@
     group, block = pl.program_id(0), pl.program_id(1)
     lanes2 = 2 * hs
 
+    chip = place_ref[0] // 2
+    w_parts = [piece.at[: w_all.shape[0]] for piece in w_refs]
+    copies = fetches(x_refs, [0, x_refs[0].shape[0]], x_all, 0, sems, n_w) + fetches(
+        w_parts, piece_rows(chip, 1, w_refs[0].shape[1], n_w), w_all, 1, sems, 0
+    )
+    late = copies.pop(1)
+
     @pl.when((group == 0) & (block == 0))
     def _():
-        chip = place_ref[0] // 2
-        w_parts = [piece.at[: w_all.shape[0]] for piece in w_refs]
-        copies = fetches(
-            w_parts, piece_rows(chip, 1, w_refs[0].shape[1], n_w), w_all, 1, sems, 0
-        ) + fetches(x_refs, [0, x_refs[0].shape[0]], x_all, 0, sems, n_w)
         for copy in copies:
             copy.start()
+        late.start()
         for copy in copies:
             copy.wait()
 
@@ -73,6 +76,12 @@
     def _():
         weight = w_all[group]
         for k in range(blocks):
+            if k == blocks // 2:
+
+                @pl.when(group == 0)
+                def _():
+                    late.wait()
+
             part = pl.ds(k * rows, rows)
             out = (mm(x_all[part, :], weight) + bias_ref[0]).astype(BF16)
             q_out[part, :] = out[:, :lanes2] * (hs**-0.5)

time: 380 us -> 380 us (level)
  no operation moved by 1% of the time
where the time goes in v2:
time: 380 us; the launch traced here: 373 us
  Pallas kernels  143 us (38%)
  waiting for transfers between devices  88 us (23%)
  starting transfers between devices  84.6 us (22%)
  other arithmetic  29.3 us (8%)
  local copies, waits for them, and re-layouts  25.3 us (7%)
    pallas_call x1, Pallas kernels, dense(): pl.pallas_call(functools.partial(dense_kernel, n_w=len(w_pieces), chunks=...  46.7 us
    pallas_call x3, Pallas kernels, attend_back(): pl.pallas_call(functools.partial(attend_back_kernel, rows=rows, hs=hs, bl...  32.4 us
    pallas_call x1, Pallas kernels, attend(): pl.pallas_call(functools.partial(attend_kernel, rows=rows, hs=hs, blocks=...  29.4 us
    ppermute x10, waiting for transfers between devices, z_step(): return lax.ppermute(x, 'tensor', [(i, i ^ k) for i in range(nt)])  29 us
    ppermute x21, waiting for transfers between devices, chip_step(): return lax.ppermute(x, 'dp', [(i, i ^ 2 * k) for i in range(ndp)])  24.7 us
    ppermute x21, starting transfers between devices, chip_step(): return lax.ppermute(x, 'dp', [(i, i ^ 2 * k) for i in range(ndp)])  22.6 us
    ppermute x1, waiting for transfers between devices, per_device(): ff_end = lax.ppermute(ff_middle, 'tensor', [(1, 0), (2, 3)])  19.4 us
    ppermute x14, starting transfers between devices, core_swap(): return lax.ppermute(x, 'dp', core_pairs)  19 us
  transfers between devices with their start and end apart: 59, of which 22 were waited for; matrix products, arithmetic and copies ran while one was open for 8% of the time, Pallas kernels for 26%

profile of v2, /device:TPU:0, one launch (start us, length us, event | category | flops | bytes accessed | tf_op | source)
XLA Modules:
  0.0 372.9 jit_solution(5248485203830179790)
XLA Ops:
  5.3 3.1 collective-permute-start
  8.4 2.6 collective-permute-start.1
  11.0 3.8 %collective-permute-done = bf16[104,768]{1,0:T(8,128)(2,1)S(1)} collective-permute-done((bf16[104,768]{1,0:T(8,128)(2,1)S(1)}, bf16[104,768]{1,0:T(8,128)(2,1)S(1)}, u32[]{:S(2)}, u32[]{:S(2)}) %collective-permute-start) | collective-permute-done | bytes 159776 | tf_op jit(solution)/shard_map/ppermute | solution.py:697
  14.9 8.3 %collective-permute-done.1 = bf16[104,768]{1,0:T(8,128)(2,1)S(1)} collective-permute-done((bf16[104,768]{1,0:T(8,128)(2,1)S(1)}, bf16[104,768]{1,0:T(8,128)(2,1)S(1)}, u32[]{:S(2)}, u32[]{:S(2)}) %collective-permute-start.1) | collective-permute-done | bytes 159776 | tf_op jit(solution)/shard_map/ppermute | solution.py:697
  24.0 2.4 collective-permute-start.4
  27.1 5.1 %collective-permute-done.4 = bf16[96,1536]{1,0:T(8,128)(2,1)S(1)} collective-permute-done((bf16[96,1536]{1,0:T(8,128)(2,1)S(1)}, bf16[96,1536]{1,0:T(8,128)(2,1)S(1)}, u32[]{:S(2)}, u32[]{:S(2)}) %collective-permute-start.4) | collective-permute-done | bytes 294944 | tf_op jit(solution)/shard_map/ppermute | solution.py:697
  41.8 19.4 %collective-permute-done.9 = bf16[2,96,1536]{2,1,0:T(8,128)(2,1)S(1)} collective-permute-done((bf16[2,96,1536]{2,1,0:T(8,128)(2,1)S(1)}, bf16[2,96,1536]{2,1,0:T(8,128)(2,1)S(1)}, u32[]{:S(2)}, u32[]{:S(2)}) %collective-permute-start.9) | collective-permute-done | bytes 589856 | tf_op jit(solution)/shard_map/ppermute | solution.py:774
  61.4 3.3 collective-permute-done.6.refs_4_
  66.4 4.8 %collective-permute-start.13 = (bf16[512,768]{1,0:T(8,128)(2,1)}, bf16[512,768]{1,0:T(8,128)(2,1)S(1)}, u32[]{:S(2)}, u32[]{:S(2)}) collective-permute-start(bf16[512,768]{1,0:T(8,128)(2,1)} %get-tuple-element.369), channel_id=1, source_target_pairs={{0,1},{1,0},{2,5},{3,4},{4,3},{5,2},{6,7},{7,6},{8,9},{9,8},{10,13... | collective-permute-start | bytes 2359304 | tf_op jit(solution)/shard_map/ppermute | solution.py:717
  76.1 2.3 pad_maximum_fusion.3.refs_3_
  78.4 6.2 %collective-permute-done.11 = bf16[2,96,1536]{2,1,0:T(8,128)(2,1)} collective-permute-done((bf16[2,96,1536]{2,1,0:T(8,128)(2,1)S(1)}, bf16[2,96,1536]{2,1,0:T(8,128)(2,1)}, u32[]{:S(2)}, u32[]{:S(2)}) %collective-permute-start.11) | collective-permute-done | bytes 589856 | tf_op jit(solution)/shard_map/ppermute | solution.py:700
  86.8 3.0 collective-permute-done.13
  92.8 2.6 collective-permute-done.15.refs_6_
  102.0 29.4 %attend.1 = (bf16[2048,384]{1,0:T(8,128)(2,1)}, bf16[2048,384]{1,0:T(8,128)(2,1)}, bf16[2048,384]{1,0:T(8,128)(2,1)}, bf16[1024,384]{1,0:T(8,128)(2,1)}, bf16[10...) custom-call(s32[6,4]{1,0:T(8,128)} %pad_add_fusion.1.pair_ref, s32[2]{0:T(128)} %pad_add_fusion.2.place_ref, ...), custom_call_target="tpu_custom_call" | custom-call | flops 1000000000 | bytes 65536 | tf_op jit(solution)/shard_map/attend/pallas_call | solution.py:135
  131.5 2.7 collective-permute-start.23
  137.9 2.2 collective-permute-done.22.refs_1_
  141.9 46.7 %dense.1 = (bf16[512,768]{1,0:T(8,128)(2,1)}, bf16[512,768]{1,0:T(8,128)(2,1)}, bf16[1024,384]{1,0:T(8,128)(2,1)}, bf16[1024,384]{1,0:T(8,128)(2,1)}, bf16[1024,...) custom-call(s32[2]{0:T(128)} %pad_add_fusion.2.place_ref, ...), custom_call_target="tpu_custom_call" | custom-call | flops 1000000000 | bytes 65536 | tf_op jit(solution)/shard_map/dense/pallas_call | solution.py:546
  190.9 2.8 copy-done.7
  195.1 7.8 %weight_grad.2 = (f32[4,2,96,768]{3,2,1,0:T(8,128)S(1)}, bf16[4,2,96,768]{3,2,1,0:T(8,128)(2,1)S(1)}, bf16[4,4,96,768]{3,2,1,0:T(8,128)(2,1)S(1)}) custom-call(s32[2]{0:T(128)S(1)} %copy-done.27, bf16[1024,768]{1,0:T(8,128)(2,1)S(1)} %copy-done.23, bf16[1024,3072]{1,0:T(8,128)(2,1)S(1)} %copy-done.7), custom_call_target="tpu_custom_call" | custom-call | flops 1000000000 | bytes 65536 | tf_op jit(solution)/shard_map/weight_grad/pallas_call | solution.py:625
  202.9 6.0 %collective-permute-start.28 = (bf16[4,4,96,768]{3,2,1,0:T(8,128)(2,1)S(1)}, bf16[4,4,96,768]{3,2,1,0:T(8,128)(2,1)S(1)}, u32[]{:S(2)}, u32[]{:S(2)}) collective-permute-start(bf16[4,4,96,768]{3,2,1,0:T(8,128)(2,1)S(1)} %get-tuple-element.214), channel_id=1, source_target_pairs={{0,4},{4,0},{8,12},{12,8},{16,20},{20,16},{24,28},{28,24},{1,5},{5... | collective-permute-start | bytes 7077896 | tf_op jit(solution)/shard_map/ppermute | solution.py:694
  211.8 9.6 %weight_grad.3 = (f32[5,2,96,768]{3,2,1,0:T(8,128)S(1)}, bf16[5,2,96,768]{3,2,1,0:T(8,128)(2,1)S(1)}, bf16[5,4,96,768]{3,2,1,0:T(8,128)(2,1)S(1)}) custom-call(s32[2]{0:T(128)S(1)} %copy-done.27, bf16[1024,768]{1,0:T(8,128)(2,1)S(1)} %copy-done.21, bf16[1024,3072]{1,0:T(8,128)(2,1)S(1)} %copy-done.8, bf16[1024,768]{1,0:T(8,128)(2,1)S(1)} %copy-done.22, ...), custom_call_target="tpu_custom_call" | custom-call | flops 1000000000 | bytes 65536 | tf_op jit(solution)/shard_map/weight_grad/pallas_call | solution.py:625
  224.2 10.7 %attend_back.3 = (bf16[2048,384]{1,0:T(8,128)(2,1)S(1)}, f32[8,128]{1,0:T(8,128)S(1)}) custom-call(s32[6,4]{1,0:T(8,128)S(1)} %copy-done.26, s32[1]{0:T(128)} %constant.127.clone.1.group_ref, bf16[2048,384]{1,0:T(8,128)(2,1)S(1)} %copy-done.3, bf16[2048,384]{1,0:T(8,128)(2,1)S(1)} %copy-done.4, bf16[2048,384]{1,0:T(8,128)(2,1)S(1)} %copy-done.5, ...), custom_call_target="tpu_custom_call" | custom-call | flops 1000000000 | bytes 65536 | tf_op jit(solution)/shard_map/attend_back/pallas_call | solution.py:233
  234.9 2.8 collective-permute-done.29
  242.9 11.0 %attend_back.4 = (bf16[2048,384]{1,0:T(8,128)(2,1)S(1)}, f32[8,128]{1,0:T(8,128)S(1)}) custom-call(s32[6,4]{1,0:T(8,128)S(1)} %copy-done.26, s32[1]{0:T(128)} %constant.128.clone.1.group_ref, bf16[2048,384]{1,0:T(8,128)(2,1)S(1)} %copy-done.3, bf16[2048,384]{1,0:T(8,128)(2,1)S(1)} %copy-done.4, bf16[2048,384]{1,0:T(8,128)(2,1)S(1)} %copy-done.5, ...), custom_call_target="tpu_custom_call" | custom-call | flops 1000000000 | bytes 65536 | tf_op jit(solution)/shard_map/attend_back/pallas_call | solution.py:233
  254.2 10.7 %attend_back.5 = (bf16[2048,384]{1,0:T(8,128)(2,1)S(1)}, f32[8,128]{1,0:T(8,128)S(1)}) custom-call(s32[6,4]{1,0:T(8,128)S(1)} %copy-done.26, s32[1]{0:T(128)} %constant.129.clone.1.group_ref, bf16[2048,384]{1,0:T(8,128)(2,1)S(1)} %copy-done.3, bf16[2048,384]{1,0:T(8,128)(2,1)S(1)} %copy-done.4, bf16[2048,384]{1,0:T(8,128)(2,1)S(1)} %copy-done.5, ...), custom_call_target="tpu_custom_call" | custom-call | flops 1000000000 | bytes 65536 | tf_op jit(solution)/shard_map/attend_back/pallas_call | solution.py:233
  274.1 10.3 %in_grad.1 = (f32[1024,768]{1,0:T(8,128)}, bf16[1024,768]{1,0:T(8,128)(2,1)}) custom-call(bf16[2048,384]{1,0:T(8,128)(2,1)} %copy-done.9, bf16[2048,384]{1,0:T(8,128)(2,1)} %copy-done.11, bf16[2048,384]{1,0:T(8,128)(2,1)} %copy-done.13, bf16[3,768,384]{2,1,0:T(8,128)(2,1)} %get-tuple-element.275.refs_3_, f32[1024,768]{1,0:T(8,128)} %get-tuple-element.276.refs_4_), custom_call_target="tpu_custom_call" | custom-call | flops 1000000000 | bytes 65536 | tf_op jit(solution)/shard_map/in_grad/pallas_call | solution.py:360
  292.7 6.7 %qkv_grads.1 = (f32[3,2,192,384]{3,2,1,0:T(8,128)S(1)}, bf16[2,2,192,384]{3,2,1,0:T(8,128)(2,1)S(1)}, bf16[1,2,192,384]{3,2,1,0:T(8,128)(2,1)S(1)}) custom-call(s32[2]{0:T(128)S(1)} %copy-done.27, bf16[2048,384]{1,0:T(8,128)(2,1)S(1)} %copy-done.10, bf16[2048,384]{1,0:T(8,128)(2,1)S(1)} %copy-done.12, bf16[2048,384]{1,0:T(8,128)(2,1)S(1)} %copy-done.14, ...), custom_call_target="tpu_custom_call" | custom-call | flops 1000000000 | bytes 65536 | tf_op jit(solution)/shard_map/qkv_grads/pallas_call | solution.py:310
  299.5 9.8 %collective-permute-done.46 = f32[16,768]{1,0:T(8,128)S(1)} collective-permute-done((f32[16,768]{1,0:T(8,128)S(1)}, f32[16,768]{1,0:T(8,128)S(1)}, u32[]{:S(2)}, u32[]{:S(2)}) %collective-permute-start.46) | collective-permute-done | bytes 49184 | tf_op jit(solution)/shard_map/ppermute | solution.py:697
  319.1 6.8 %collective-permute-done.47 = bf16[2,2,192,384]{3,2,0,1:T(8,128)(2,1)} collective-permute-done((bf16[2,2,192,384]{3,2,0,1:T(8,128)(2,1)}, bf16[2,2,192,384]{3,2,0,1:T(8,128)(2,1)}, u32[]{:S(2)}, u32[]{:S(2)}) %collective-permute-start.47) | collective-permute-done | bytes 589856 | tf_op jit(solution)/shard_map/ppermute | solution.py:700
  338.1 8.1 %collective-permute-start.55 = (f32[16,768]{1,0:T(8,128)S(1)}, f32[16,768]{1,0:T(8,128)S(1)}, u32[]{:S(2)}, u32[]{:S(2)}) collective-permute-start(f32[16,768]{1,0:T(8,128)S(1)} %copy-done.44), channel_id=1, source_target_pairs={{0,4},{4,0},{8,12},{12,8},{16,20},{20,16},{24,28},{28,24},{1,5},{5... | collective-permute-start | bytes 147464 | tf_op jit(solution)/shard_map/ppermute | solution.py:694
  346.9 9.2 %collective-permute-start.52 = (bf16[96,576]{1,0:T(8,128)(2,1)S(1)}, bf16[96,576]{1,0:T(8,128)(2,1)S(1)}, u32[]{:S(2)}, u32[]{:S(2)}) collective-permute-start(bf16[96,576]{1,0:T(8,128)(2,1)S(1)} %broadcast_select_fusion.16), channel_id=1, source_target_pairs={{0,1},{1,0},{2,5},{3,4},{4,3},{5,2},{6,7},{7,6},{8,9},{9,8},{10,13... | collective-permute-start | bytes 331784 | tf_op jit(solution)/shard_map/ppermute | solution.py:1054
  356.0 3.3 collective-permute-start.53
  (403 shorter events, 106.6 us)
Async XLA Ops:
  8.4 14.8 %collective-permute-start.1 = (bf16[104,768]{1,0:T(8,128)(2,1)S(1)}, bf16[104,768]{1,0:T(8,128)(2,1)S(1)}, u32[]{:S(2)}, u32[]{:S(2)}) collective-permute-start(bf16[104,768]{1,0:T(8,128)(2,1)S(1)} %pad_maximum_fusion.11), channel_id=1, source_target_pairs={{0,2},{1,3},{2,0},{3,1},{4,6},{5,7},{6,4},{7,5},{8,10},{9,11},{10,... | collective-permute-start | bytes 479240 | tf_op jit(solution)/shard_map/ppermute | solution.py:697
  35.3 26.1 %collective-permute-start.5 = (bf16[4,192,384]{2,1,0:T(8,128)(2,1)S(1)}, bf16[4,192,384]{2,1,0:T(8,128)(2,1)S(1)}, u32[]{:S(2)}, u32[]{:S(2)}) collective-permute-start(bf16[4,192,384]{2,1,0:T(8,128)(2,1)S(1)} %maximum_select_fusion.refs_2_), channel_id=1, source_target_pairs={{0,8},{4,12},{8,0},{12,4},{16,24},{20,28},{24,16},{28,20},{1,9},{5... | collective-permute-start | bytes 1769480 | tf_op jit(solution)/shard_map/ppermute | solution.py:700
  36.8 28.0 %collective-permute-start.6 = (bf16[4,192,384]{2,1,0:T(8,128)(2,1)S(1)}, bf16[4,192,384]{2,1,0:T(8,128)(2,1)S(1)}, u32[]{:S(2)}, u32[]{:S(2)}) collective-permute-start(bf16[4,192,384]{2,1,0:T(8,128)(2,1)S(1)} %maximum_select_fusion.refs_2_), channel_id=1, source_target_pairs={{0,16},{4,20},{8,24},{12,28},{16,0},{20,4},{24,8},{28,12},{1,17},{... | collective-permute-start | bytes 1769480 | tf_op jit(solution)/shard_map/ppermute | solution.py:700
  38.3 26.4 %collective-permute-start.7 = (bf16[4,192,384]{2,1,0:T(8,128)(2,1)S(1)}, bf16[4,192,384]{2,1,0:T(8,128)(2,1)S(1)}, u32[]{:S(2)}, u32[]{:S(2)}) collective-permute-start(bf16[4,192,384]{2,1,0:T(8,128)(2,1)S(1)} %maximum_select_fusion.refs_2_), channel_id=1, source_target_pairs={{0,24},{4,28},{8,16},{12,20},{16,8},{20,12},{24,0},{28,4},{1,25},{... | collective-permute-start | bytes 1769480 | tf_op jit(solution)/shard_map/ppermute | solution.py:700
  38.8 22.4 %collective-permute-start.9 = (bf16[2,96,1536]{2,1,0:T(8,128)(2,1)S(1)}, bf16[2,96,1536]{2,1,0:T(8,128)(2,1)S(1)}, u32[]{:S(2)}, u32[]{:S(2)}) collective-permute-start(bf16[2,96,1536]{2,1,0:T(8,128)(2,1)S(1)} %collective-permute-done.8), channel_id=1, source_target_pairs={{1,0},{2,3},{5,4},{6,7},{9,8},{10,11},{13,12},{14,15},{17,16},{18,... | collective-permute-start | bytes 1769480 | tf_op jit(solution)/shard_map/ppermute | solution.py:774
  41.1 23.7 %collective-permute-start.10 = (bf16[512,768]{1,0:T(8,128)(2,1)S(1)}, bf16[512,768]{1,0:T(8,128)(2,1)S(1)}, u32[]{:S(2)}, u32[]{:S(2)}) collective-permute-start(bf16[512,768]{1,0:T(8,128)(2,1)S(1)} %get-tuple-element.370), channel_id=1, source_target_pairs={{0,0},{1,1},{2,4},{3,5},{4,2},{5,3},{6,6},{7,7},{8,8},{9,9},{10,12... | collective-permute-start | bytes 2359304 | tf_op jit(solution)/shard_map/ppermute | solution.py:717
  66.4 23.4 %collective-permute-start.13 = (bf16[512,768]{1,0:T(8,128)(2,1)}, bf16[512,768]{1,0:T(8,128)(2,1)S(1)}, u32[]{:S(2)}, u32[]{:S(2)}) collective-permute-start(bf16[512,768]{1,0:T(8,128)(2,1)} %get-tuple-element.369), channel_id=1, source_target_pairs={{0,1},{1,0},{2,5},{3,4},{4,3},{5,2},{6,7},{7,6},{8,9},{9,8},{10,13... | collective-permute-start | bytes 2359304 | tf_op jit(solution)/shard_map/ppermute | solution.py:717
  91.1 40.4 %collective-permute-start.18 = (bf16[2,2,96,1536]{3,2,1,0:T(8,128)(2,1)}, bf16[2,2,96,1536]{3,2,1,0:T(8,128)(2,1)}, u32[]{:S(2)}, u32[]{:S(2)}) collective-permute-start(bf16[2,2,96,1536]{3,2,1,0:T(8,128)(2,1)} %pad_maximum_fusion.2.refs_2_), channel_id=1, source_target_pairs={{0,16},{4,20},{8,24},{12,28},{16,0},{20,4},{24,8},{28,12},{1,17},{... | collective-permute-start | bytes 3538952 | tf_op jit(solution)/shard_map/ppermute | solution.py:700
  91.6 39.9 %collective-permute-start.19 = (bf16[2,2,96,1536]{3,2,1,0:T(8,128)(2,1)}, bf16[2,2,96,1536]{3,2,1,0:T(8,128)(2,1)}, u32[]{:S(2)}, u32[]{:S(2)}) collective-permute-start(bf16[2,2,96,1536]{3,2,1,0:T(8,128)(2,1)} %pad_maximum_fusion.3.refs_3_), channel_id=1, source_target_pairs={{0,8},{4,12},{8,0},{12,4},{16,24},{20,28},{24,16},{28,20},{1,9},{5... | collective-permute-start | bytes 3538952 | tf_op jit(solution)/shard_map/ppermute | solution.py:700
  97.1 34.4 %collective-permute-start.20 = (bf16[512,768]{1,0:T(8,128)(2,1)}, bf16[512,768]{1,0:T(8,128)(2,1)S(1)}, u32[]{:S(2)}, u32[]{:S(2)}) collective-permute-start(bf16[512,768]{1,0:T(8,128)(2,1)} %get-tuple-element.197), channel_id=1, source_target_pairs={{0,0},{1,1},{2,4},{3,5},{4,2},{5,3},{6,6},{7,7},{8,8},{9,9},{10,12... | collective-permute-start | bytes 2359304 | tf_op jit(solution)/shard_map/ppermute | solution.py:717
  98.9 32.6 %collective-permute-start.21 = (bf16[512,768]{1,0:T(8,128)(2,1)}, bf16[512,768]{1,0:T(8,128)(2,1)S(1)}, u32[]{:S(2)}, u32[]{:S(2)}) collective-permute-start(bf16[512,768]{1,0:T(8,128)(2,1)} %get-tuple-element.198), channel_id=1, source_target_pairs={{0,1},{1,0},{2,5},{3,4},{4,3},{5,2},{6,7},{7,6},{8,9},{9,8},{10,13... | collective-permute-start | bytes 2359304 | tf_op jit(solution)/shard_map/ppermute | solution.py:717
  188.6 20.3 %collective-permute-start.26 = (bf16[1024,384]{1,0:T(8,128)(2,1)}, bf16[1024,384]{1,0:T(8,128)(2,1)S(1)}, u32[]{:S(2)}, u32[]{:S(2)}) collective-permute-start(bf16[1024,384]{1,0:T(8,128)(2,1)} %get-tuple-element.215), channel_id=1, source_target_pairs={{0,4},{4,0},{8,12},{12,8},{16,20},{20,16},{24,28},{28,24},{1,5},{5... | collective-permute-start | bytes 2359304 | tf_op jit(solution)/shard_map/ppermute | solution.py:694
  189.1 32.3 %collective-permute-start.27 = (bf16[512,768]{1,0:T(8,128)(2,1)}, bf16[512,768]{1,0:T(8,128)(2,1)S(1)}, u32[]{:S(2)}, u32[]{:S(2)}) collective-permute-start(bf16[512,768]{1,0:T(8,128)(2,1)} %get-tuple-element.222), channel_id=1, source_target_pairs={{0,0},{1,1},{4,2},{5,3},{2,4},{3,5},{6,6},{7,7},{8,8},{9,9},{12,10... | collective-permute-start | bytes 2359304 | tf_op jit(solution)/shard_map/ppermute | solution.py:854
  202.9 18.6 %collective-permute-start.28 = (bf16[4,4,96,768]{3,2,1,0:T(8,128)(2,1)S(1)}, bf16[4,4,96,768]{3,2,1,0:T(8,128)(2,1)S(1)}, u32[]{:S(2)}, u32[]{:S(2)}) collective-permute-start(bf16[4,4,96,768]{3,2,1,0:T(8,128)(2,1)S(1)} %get-tuple-element.214), channel_id=1, source_target_pairs={{0,4},{4,0},{8,12},{12,8},{16,20},{20,16},{24,28},{28,24},{1,5},{5... | collective-permute-start | bytes 7077896 | tf_op jit(solution)/shard_map/ppermute | solution.py:694
  221.4 16.6 %collective-permute-start.31 = (bf16[5,4,96,768]{3,2,1,0:T(8,128)(2,1)S(1)}, bf16[5,4,96,768]{3,2,1,0:T(8,128)(2,1)S(1)}, u32[]{:S(2)}, u32[]{:S(2)}) collective-permute-start(bf16[5,4,96,768]{3,2,1,0:T(8,128)(2,1)S(1)} %get-tuple-element.239), channel_id=1, source_target_pairs={{0,4},{4,0},{8,12},{12,8},{16,20},{20,16},{24,28},{28,24},{1,5},{5... | collective-permute-start | bytes 8847368 | tf_op jit(solution)/shard_map/ppermute | solution.py:694
  221.9 15.8 %collective-permute-start.29 = (bf16[2,2,96,768]{3,2,0,1:T(8,128)(2,1)S(1)}, bf16[2,2,96,768]{3,2,0,1:T(8,128)(2,1)S(1)}, u32[]{:S(2)}, u32[]{:S(2)}) collective-permute-start(bf16[2,2,96,768]{3,2,0,1:T(8,128)(2,1)S(1)} %get-tuple-element.237), channel_id=1, source_target_pairs={{0,8},{4,12},{8,0},{12,4},{16,24},{20,28},{24,16},{28,20},{1,9},{5... | collective-permute-start | bytes 1769480 | tf_op jit(solution)/shard_map/ppermute | solution.py:700
  222.6 15.4 %collective-permute-start.30 = (bf16[2,2,96,768]{3,2,0,1:T(8,128)(2,1)S(1)}, bf16[2,2,96,768]{3,2,0,1:T(8,128)(2,1)S(1)}, u32[]{:S(2)}, u32[]{:S(2)}) collective-permute-start(bf16[2,2,96,768]{3,2,0,1:T(8,128)(2,1)S(1)} %get-tuple-element.238), channel_id=1, source_target_pairs={{0,16},{4,20},{8,24},{12,28},{16,0},{20,4},{24,8},{28,12},{1,17},{... | collective-permute-start | bytes 1769480 | tf_op jit(solution)/shard_map/ppermute | solution.py:700
  223.8 30.2 %collective-permute-start.34 = (bf16[512,768]{1,0:T(8,128)(2,1)S(1)}, bf16[512,768]{1,0:T(8,128)(2,1)S(1)}, u32[]{:S(2)}, u32[]{:S(2)}) collective-permute-start(bf16[512,768]{1,0:T(8,128)(2,1)S(1)} %copy-done.60), channel_id=1, source_target_pairs={{1,0},{0,1},{5,2},{4,3},{3,4},{2,5},{7,6},{6,7},{9,8},{8,9},{13,10... | collective-permute-start | bytes 2359304 | tf_op jit(solution)/shard_map/ppermute | solution.py:943
  238.8 15.1 %collective-permute-start.32 = (bf16[2,96,768]{2,1,0:T(8,128)(2,1)S(1)}, bf16[2,96,768]{2,1,0:T(8,128)(2,1)S(1)}, u32[]{:S(2)}, u32[]{:S(2)}) collective-permute-start(bf16[2,96,768]{2,1,0:T(8,128)(2,1)S(1)} %get-tuple-element.247), channel_id=1, source_target_pairs={{0,16},{4,20},{8,24},{12,28},{16,0},{20,4},{24,8},{28,12},{1,17},{... | collective-permute-start | bytes 884744 | tf_op jit(solution)/shard_map/ppermute | solution.py:700
  240.0 14.0 %collective-permute-start.33 = (bf16[2,96,768]{2,1,0:T(8,128)(2,1)S(1)}, bf16[2,96,768]{2,1,0:T(8,128)(2,1)S(1)}, u32[]{:S(2)}, u32[]{:S(2)}) collective-permute-start(bf16[2,96,768]{2,1,0:T(8,128)(2,1)S(1)} %fusion.18), channel_id=1, source_target_pairs={{0,8},{4,12},{8,0},{12,4},{16,24},{20,28},{24,16},{28,20},{1,9},{5... | collective-permute-start | bytes 884744 | tf_op jit(solution)/shard_map/ppermute | solution.py:700
  240.6 26.3 %collective-permute-start.35 = (bf16[3,2,96,768]{3,2,0,1:T(8,128)(2,1)S(1)}, bf16[3,2,96,768]{3,2,0,1:T(8,128)(2,1)S(1)}, u32[]{:S(2)}, u32[]{:S(2)}) collective-permute-start(bf16[3,2,96,768]{3,2,0,1:T(8,128)(2,1)S(1)} %add_convert_fusion), channel_id=1, source_target_pairs={{0,8},{4,12},{8,0},{12,4},{16,24},{20,28},{24,16},{28,20},{1,9},{5... | collective-permute-start | bytes 2654216 | tf_op jit(solution)/shard_map/ppermute | solution.py:700
  242.0 25.0 %collective-permute-start.36 = (bf16[2,2,96,768]{3,2,0,1:T(8,128)(2,1)S(1)}, bf16[2,2,96,768]{3,2,0,1:T(8,128)(2,1)S(1)}, u32[]{:S(2)}, u32[]{:S(2)}) collective-permute-start(bf16[2,2,96,768]{3,2,0,1:T(8,128)(2,1)S(1)} %add_convert_fusion.3), channel_id=1, source_target_pairs={{0,16},{4,20},{8,24},{12,28},{16,0},{20,4},{24,8},{28,12},{1,17},{... | collective-permute-start | bytes 1769480 | tf_op jit(solution)/shard_map/ppermute | solution.py:700
  268.3 16.2 %collective-permute-start.40 = (bf16[3,96,768]{2,1,0:T(8,128)(2,1)S(1)}, bf16[3,96,768]{2,1,0:T(8,128)(2,1)}, u32[]{:S(2)}, u32[]{:S(2)}) collective-permute-start(bf16[3,96,768]{2,1,0:T(8,128)(2,1)S(1)} %get-tuple-element.281), channel_id=1, source_target_pairs={{0,16},{4,20},{8,24},{12,28},{16,0},{20,4},{24,8},{28,12},{1,17},{... | collective-permute-start | bytes 1327112 | tf_op jit(solution)/shard_map/ppermute | solution.py:700
  269.3 15.2 %collective-permute-start.41 = (bf16[2,96,768]{2,1,0:T(8,128)(2,1)S(1)}, bf16[2,96,768]{2,1,0:T(8,128)(2,1)S(1)}, u32[]{:S(2)}, u32[]{:S(2)}) collective-permute-start(bf16[2,96,768]{2,1,0:T(8,128)(2,1)S(1)} %fusion.19), channel_id=1, source_target_pairs={{0,8},{4,12},{8,0},{12,4},{16,24},{20,28},{24,16},{28,20},{1,9},{5... | collective-permute-start | bytes 884744 | tf_op jit(solution)/shard_map/ppermute | solution.py:700
  288.2 21.1 %collective-permute-start.45 = (bf16[96,1920]{1,0:T(8,128)(2,1)S(1)}, bf16[96,1920]{1,0:T(8,128)(2,1)S(1)}, u32[]{:S(2)}, u32[]{:S(2)}) collective-permute-start(bf16[96,1920]{1,0:T(8,128)(2,1)S(1)} %pad_maximum_fusion.6), channel_id=1, source_target_pairs={{0,2},{1,3},{2,0},{3,1},{4,6},{5,7},{6,4},{7,5},{8,10},{9,11},{10,... | collective-permute-start | bytes 1105928 | tf_op jit(solution)/shard_map/ppermute | solution.py:697
  291.0 18.3 %collective-permute-start.46 = (f32[16,768]{1,0:T(8,128)S(1)}, f32[16,768]{1,0:T(8,128)S(1)}, u32[]{:S(2)}, u32[]{:S(2)}) collective-permute-start(f32[16,768]{1,0:T(8,128)S(1)} %add.284), channel_id=1, source_target_pairs={{0,2},{1,3},{2,0},{3,1},{4,6},{5,7},{6,4},{7,5},{8,10},{9,11},{10,... | collective-permute-start | bytes 147464 | tf_op jit(solution)/shard_map/ppermute | solution.py:697
  310.3 15.6 %collective-permute-start.47 = (bf16[2,2,192,384]{3,2,0,1:T(8,128)(2,1)}, bf16[2,2,192,384]{3,2,0,1:T(8,128)(2,1)}, u32[]{:S(2)}, u32[]{:S(2)}) collective-permute-start(bf16[2,2,192,384]{3,2,0,1:T(8,128)(2,1)} %copy.94), channel_id=1, source_target_pairs={{0,8},{4,12},{8,0},{12,4},{16,24},{20,28},{24,16},{28,20},{1,9},{5... | collective-permute-start | bytes 1769480 | tf_op jit(solution)/shard_map/ppermute | solution.py:700
  311.8 20.0 %collective-permute-start.43 = (bf16[512,768]{1,0:T(8,128)(2,1)}, bf16[512,768]{1,0:T(8,128)(2,1)S(1)}, u32[]{:S(2)}, u32[]{:S(2)}) collective-permute-start(bf16[512,768]{1,0:T(8,128)(2,1)} %get-tuple-element.294), channel_id=1, source_target_pairs={{0,0},{1,1},{4,2},{5,3},{2,4},{3,5},{6,6},{7,7},{8,8},{9,9},{12,10... | collective-permute-start | bytes 2359304 | tf_op jit(solution)/shard_map/ppermute | solution.py:997
  313.6 20.2 %collective-permute-start.44 = (bf16[512,768]{1,0:T(8,128)(2,1)}, bf16[512,768]{1,0:T(8,128)(2,1)}, u32[]{:S(2)}, u32[]{:S(2)}) collective-permute-start(bf16[512,768]{1,0:T(8,128)(2,1)} %get-tuple-element.295), channel_id=1, source_target_pairs={{1,0},{0,1},{5,2},{4,3},{3,4},{2,5},{7,6},{6,7},{9,8},{8,9},{13,10... | collective-permute-start | bytes 2359304 | tf_op jit(solution)/shard_map/ppermute | solution.py:997
  338.1 22.5 %collective-permute-start.55 = (f32[16,768]{1,0:T(8,128)S(1)}, f32[16,768]{1,0:T(8,128)S(1)}, u32[]{:S(2)}, u32[]{:S(2)}) collective-permute-start(f32[16,768]{1,0:T(8,128)S(1)} %copy-done.44), channel_id=1, source_target_pairs={{0,4},{4,0},{8,12},{12,8},{16,20},{20,16},{24,28},{28,24},{1,5},{5... | collective-permute-start | bytes 147464 | tf_op jit(solution)/shard_map/ppermute | solution.py:694
  346.2 20.2 %collective-permute-start.51 = (bf16[96,576]{1,0:T(8,128)(2,1)S(1)}, bf16[96,576]{1,0:T(8,128)(2,1)S(1)}, u32[]{:S(2)}, u32[]{:S(2)}) collective-permute-start(bf16[96,576]{1,0:T(8,128)(2,1)S(1)} %broadcast_select_fusion.17), channel_id=1, source_target_pairs={{0,0},{1,1},{2,4},{3,5},{4,2},{5,3},{6,6},{7,7},{8,8},{9,9},{10,12... | collective-permute-start | bytes 331784 | tf_op jit(solution)/shard_map/ppermute | solution.py:1054
  346.9 19.6 %collective-permute-start.52 = (bf16[96,576]{1,0:T(8,128)(2,1)S(1)}, bf16[96,576]{1,0:T(8,128)(2,1)S(1)}, u32[]{:S(2)}, u32[]{:S(2)}) collective-permute-start(bf16[96,576]{1,0:T(8,128)(2,1)S(1)} %broadcast_select_fusion.16), channel_id=1, source_target_pairs={{0,1},{1,0},{2,5},{3,4},{4,3},{5,2},{6,7},{7,6},{8,9},{9,8},{10,13... | collective-permute-start | bytes 331784 | tf_op jit(solution)/shard_map/ppermute | solution.py:1054
  (94 other events, 719.8 us)
